TPU v7x, 32 devices: a whole 2x2x4 slice. The times are simulated.
32 devices in a mesh: dp: 8 (over y, x, core), tensor: 4 (over z).
Axes of the slice: x: 2, y: 2, z: 4, core: 2. Of those that a mesh axis runs over, the one named last changes fastest.
Arguments:
- tokens: bfloat16 [16384, 640], P(('dp', 'tensor')), may hold values from -6 to 6
- segments: int32 [16384], P('dp'), may hold values from 0 to 10, as said below
- positions: int32 [16384], P('dp'), may hold values from 0 to 1999, as said below
- norm_gains: bfloat16 [4, 640], P(None, 'dp'), may hold values from 0.099609375 to 1.8984375
- qk_gains: bfloat16 [2, 256], P(None, 'dp'), may hold values from 0.099609375 to 1.8984375
- q_weight: bfloat16 [640, 1024], P('dp', 'tensor'), may hold values from -0.25 to 0.25
- kv_weight: bfloat16 [640, 512], P('dp'), may hold values from -0.25 to 0.25
- out_weight: bfloat16 [1024, 640], P('tensor', 'dp'), may hold values from -0.1875 to 0.1875
- gate_weight: bfloat16 [640, 2048], P('dp', 'tensor'), may hold values from -0.25 to 0.25
- up_weight: bfloat16 [640, 2048], P('dp', 'tensor'), may hold values from -0.25 to 0.25
- down_weight: bfloat16 [2048, 640], P('tensor', 'dp'), may hold values from -0.125 to 0.125
- cotangent: bfloat16 [16384, 640], P(('dp', 'tensor')), may hold values from -6 to 6
Outputs:
- block_out: bfloat16 [16384, 640], P(('dp', 'tensor'))
- tokens_grad: float32 [16384, 640], P(('dp', 'tensor'))
- norm_gains_grad: float32 [4, 640], P(None, 'dp')
- qk_gains_grad: float32 [2, 256], P(None, 'dp')
- q_weight_grad: float32 [640, 1024], P('dp', 'tensor')
- kv_weight_grad: float32 [640, 512], P('dp')
- out_weight_grad: float32 [1024, 640], P('tensor', 'dp')
- gate_weight_grad: float32 [640, 2048], P('dp', 'tensor')
- up_weight_grad: float32 [640, 2048], P('dp', 'tensor')
- down_weight_grad: float32 [2048, 640], P('tensor', 'dp')
Inputs may be any that keep to these rules, and one draw needn't show every extreme that they name: `segments`: within each sequence of 2048 tokens the segment numbers start at 0 and rise by one at each new document; every document except the last of its sequence holds between 200 and 2000 tokens. `positions`: each token's place within its document, 0 at the document's first token.
All inputs are finite; a program needn't handle non-finite values.
Results may differ from a plain program's by a relative error of at most 0.018.
Values may be sent and summed in bfloat16 or wider, within the bound.
A program may use at most 128 MiB of HBM per device.

v0:
```python
import jax
import jax.numpy as jnp
from jax import lax
from jax.sharding import PartitionSpec as P

WINDOW = 512
LEN = 2048


EPSILON = 1e-06
ROPE_BASE = 10000.0
GELU_SCALE = 0.7978845608028654


def norm_rows(values, gain_row):
    return (
        values * lax.rsqrt(jnp.mean(values * values, axis=-1, keepdims=True) + EPSILON) * gain_row
    )


def norm_back(values, gain_row, grad_out):
    inv_rms = lax.rsqrt(jnp.mean(values * values, axis=-1, keepdims=True) + EPSILON)
    weighted = grad_out * gain_row
    inner_mean = jnp.mean(values * weighted, axis=-1, keepdims=True)
    return (
        inv_rms * weighted - values * inv_rms * inv_rms * inv_rms * inner_mean,
        grad_out * values * inv_rms,
    )


def rotate(values, cosine_table, sine_table):
    half_width = values.shape[-1] // 2
    first_half = values[..., :half_width]
    second_half = values[..., half_width:]
    return jnp.concatenate(
        [
            first_half * cosine_table - second_half * sine_table,
            second_half * cosine_table + first_half * sine_table,
        ],
        axis=-1,
    )


def geglu(gate_pre, up_pre):
    inner_term = GELU_SCALE * (gate_pre + 0.044715 * gate_pre * gate_pre * gate_pre)
    return 0.5 * gate_pre * (1.0 + jnp.tanh(inner_term)) * up_pre


def dot_plain(left_side, right_side):
    return jnp.dot(left_side, right_side, preferred_element_type=jnp.float32)


def dot_last(left_side, right_side):
    return lax.dot_general(
        left_side, right_side, (((1,), (1,)), ((), ())), preferred_element_type=jnp.float32
    )


def dot_first(left_side, right_side):
    return lax.dot_general(
        left_side, right_side, (((0,), (0,)), ((), ())), preferred_element_type=jnp.float32
    )


def key_blocks(values, window_rows, fill_value):
    padding = jnp.full((window_rows,) + values.shape[1:], fill_value, values.dtype)
    padded = jnp.concatenate([padding, values], axis=0)
    block_count = values.shape[0] // window_rows
    block_shape = (block_count, window_rows) + values.shape[1:]
    return jnp.concatenate(
        [padded[:-window_rows].reshape(block_shape), padded[window_rows:].reshape(block_shape)],
        axis=1,
    )


def fold_keys(block_parts, window_rows):
    all_rows = block_parts.shape[0] * window_rows
    head_width = block_parts.shape[2]
    later_part = block_parts[:, window_rows:].reshape(all_rows, head_width)
    earlier_part = jnp.concatenate(
        [
            block_parts[1:, :window_rows].reshape(all_rows - window_rows, head_width),
            jnp.zeros((window_rows, head_width), jnp.float32),
        ],
        axis=0,
    )
    return later_part + earlier_part


def per_device(
    tokens,
    segments,
    positions,
    norm_gains,
    qk_gains,
    q_weight,
    kv_weight,
    out_weight,
    gate_weight,
    up_weight,
    down_weight,
    cotangent,
):
    gain_table, qk_table, w_query, w_keyval, w_out, w_gate, w_up, w_down = (
        lax.all_gather(norm_gains, "dp", axis=1, tiled=True),
        lax.all_gather(qk_gains, "dp", axis=1, tiled=True),
        lax.all_gather(q_weight, "dp", axis=0, tiled=True),
        lax.all_gather(kv_weight, "dp", axis=0, tiled=True),
        lax.all_gather(out_weight, "dp", axis=1, tiled=True),
        lax.all_gather(gate_weight, "dp", axis=0, tiled=True),
        lax.all_gather(up_weight, "dp", axis=0, tiled=True),
        lax.all_gather(down_weight, "dp", axis=1, tiled=True),
    )
    gain_table = gain_table.astype(jnp.float32)
    qk_table = qk_table.astype(jnp.float32)
    own_input = tokens.astype(jnp.float32)
    input_rows = lax.all_gather(tokens, "tensor", axis=0, tiled=True)
    all_rows = input_rows.shape[0]
    head_width = qk_table.shape[1]
    normed = norm_rows(input_rows.astype(jnp.float32), gain_table[0]).astype(jnp.bfloat16)
    query_raw = dot_plain(normed, w_query)
    keyval_raw = dot_plain(normed, w_keyval)
    half_width = head_width // 2
    frequency = ROPE_BASE ** (-jnp.arange(half_width, dtype=jnp.float32) * 2.0 / head_width)
    angles = positions.astype(jnp.float32)[:, None] * frequency[None, :]
    cosine_table = jnp.cos(angles)
    sine_table = jnp.sin(angles)

    def prepare(raw_part, gain_row):
        return rotate(norm_rows(raw_part, gain_row), cosine_table, sine_table)

    query_rot, query_back = jax.vjp(prepare, query_raw, qk_table[0])
    key_rot, key_back = jax.vjp(prepare, keyval_raw[:, :head_width], qk_table[1])
    queries = query_rot.astype(jnp.bfloat16)
    key_rows = key_rot.astype(jnp.bfloat16)
    value_rows = keyval_raw[:, head_width:].astype(jnp.bfloat16)
    block_count = all_rows // WINDOW
    doc_keys = segments + jnp.arange(all_rows, dtype=jnp.int32) // LEN * LEN
    offsets = jnp.arange(WINDOW)[:, None] + WINDOW - jnp.arange(2 * WINDOW)[None, :]
    near_mask = (offsets >= 0) & (offsets < WINDOW)
    score_scale = head_width ** (-0.5)
    query_blocks = queries.reshape(block_count, WINDOW, head_width)
    key_parts = key_blocks(key_rows, WINDOW, 0)
    value_parts = key_blocks(value_rows, WINDOW, 0)
    query_docs = doc_keys.reshape(block_count, WINDOW)
    key_docs = key_blocks(doc_keys, WINDOW, -1)

    def block_scores(query_part, key_part, doc_query, doc_key):
        raw_scores = dot_last(query_part, key_part) * score_scale
        allowed = near_mask & (doc_query[:, None] == doc_key[None, :])
        return jnp.where(allowed, raw_scores, -1000000000.0)

    def attend(block_item):
        query_part, key_part, value_part, doc_query, doc_key = block_item
        masked = block_scores(query_part, key_part, doc_query, doc_key)
        row_max = jnp.max(masked, axis=1, keepdims=True)
        exponent = jnp.exp(masked - row_max)
        row_total = jnp.sum(exponent, axis=1, keepdims=True)
        probabilities = (exponent / row_total).astype(jnp.bfloat16)
        return (dot_plain(probabilities, value_part), (row_max + jnp.log(row_total))[:, 0])

    context_blocks, lse_blocks = lax.map(
        attend, (query_blocks, key_parts, value_parts, query_docs, key_docs)
    )
    context = context_blocks.reshape(all_rows, head_width).astype(jnp.bfloat16)
    attn_own = lax.psum_scatter(
        dot_plain(context, w_out), "tensor", scatter_dimension=0, tiled=True
    )
    residual = own_input + norm_rows(attn_own, gain_table[1])
    ffn_in = norm_rows(residual, gain_table[2]).astype(jnp.bfloat16)
    ffn_rows = lax.all_gather(ffn_in, "tensor", axis=0, tiled=True)
    gate_pre = dot_plain(ffn_rows, w_gate)
    up_pre = dot_plain(ffn_rows, w_up)
    hidden_value, gelu_back = jax.vjp(geglu, gate_pre, up_pre)
    hidden = hidden_value.astype(jnp.bfloat16)
    ffn_out = lax.psum_scatter(dot_plain(hidden, w_down), "tensor", scatter_dimension=0, tiled=True)
    block_out = (residual + norm_rows(ffn_out, gain_table[3])).astype(jnp.bfloat16)
    top_grad = cotangent.astype(jnp.float32)
    ffn_grad_value, post_gain_rows = norm_back(ffn_out, gain_table[3], top_grad)
    ffn_grad = ffn_grad_value.astype(jnp.bfloat16)
    ffn_grad_rows = lax.all_gather(ffn_grad, "tensor", axis=0, tiled=True)
    hidden_grad = dot_last(ffn_grad_rows, w_down)
    gate_grad_value, up_grad_value = gelu_back(hidden_grad)
    gate_grad = gate_grad_value.astype(jnp.bfloat16)
    up_grad = up_grad_value.astype(jnp.bfloat16)
    ffn_in_grad = lax.psum_scatter(
        dot_last(gate_grad, w_gate) + dot_last(up_grad, w_up),
        "tensor",
        scatter_dimension=0,
        tiled=True,
    )
    gate_wgrad = dot_first(ffn_rows, gate_grad)
    up_wgrad = dot_first(ffn_rows, up_grad)
    down_wgrad = dot_first(hidden, ffn_grad_rows)
    residual_part, pre_ffn_rows = norm_back(residual, gain_table[2], ffn_in_grad)
    residual_grad = top_grad + residual_part
    attn_grad_value, post_attn_rows = norm_back(attn_own, gain_table[1], residual_grad)
    attn_grad = lax.all_gather(attn_grad_value.astype(jnp.bfloat16), "tensor", axis=0, tiled=True)
    context_grad = dot_last(attn_grad, w_out).astype(jnp.bfloat16)
    out_wgrad = dot_first(context, attn_grad)
    context_grad_blocks = context_grad.reshape(block_count, WINDOW, head_width)

    def attend_back(block_item):
        query_part, key_part, value_part, doc_query, doc_key, lse_part, grad_part = block_item
        masked = block_scores(query_part, key_part, doc_query, doc_key)
        probabilities = jnp.exp(masked - lse_part[:, None])
        prob_grad = dot_last(grad_part, value_part)
        row_delta = jnp.sum(probabilities * prob_grad, axis=1, keepdims=True)
        score_grad = (probabilities * (prob_grad - row_delta) * score_scale).astype(jnp.bfloat16)
        return (
            dot_plain(score_grad, key_part),
            dot_first(score_grad, query_part),
            dot_first(probabilities.astype(jnp.bfloat16), grad_part),
        )

    query_grad_blocks, key_grad_blocks, value_grad_blocks = lax.map(
        attend_back,
        (
            query_blocks,
            key_parts,
            value_parts,
            query_docs,
            key_docs,
            lse_blocks,
            context_grad_blocks,
        ),
    )
    query_grad = query_grad_blocks.reshape(all_rows, head_width)
    key_grad = fold_keys(key_grad_blocks, WINDOW)
    value_grad = fold_keys(value_grad_blocks, WINDOW)
    query_raw_grad, query_gain_grad = query_back(query_grad)
    key_raw_grad, key_gain_grad = key_back(key_grad)
    query_raw_low = query_raw_grad.astype(jnp.bfloat16)
    keyval_low = jnp.concatenate([key_raw_grad, value_grad], axis=1).astype(jnp.bfloat16)
    normed_grad = lax.psum_scatter(
        (dot_last(query_raw_low, w_query) + dot_last(keyval_low, w_keyval)).astype(jnp.bfloat16),
        "tensor",
        scatter_dimension=0,
        tiled=True,
    ).astype(jnp.float32)
    input_part, pre_attn_rows = norm_back(own_input, gain_table[0], normed_grad)
    tokens_grad = residual_grad + input_part
    query_wgrad = dot_first(normed, query_raw_low)
    keyval_wgrad = dot_first(normed, keyval_low)
    gain_grads = jnp.stack(
        [
            jnp.sum(pre_attn_rows, axis=0),
            jnp.sum(post_attn_rows, axis=0),
            jnp.sum(pre_ffn_rows, axis=0),
            jnp.sum(post_gain_rows, axis=0),
        ]
    )
    qk_grads = jnp.stack([query_gain_grad, key_gain_grad])
    keyval_wgrad, gain_grads, qk_grads = (
        lax.psum(keyval_wgrad.astype(jnp.bfloat16), "tensor").astype(jnp.float32),
        lax.psum(gain_grads.astype(jnp.bfloat16), "tensor").astype(jnp.float32),
        lax.psum(qk_grads.astype(jnp.bfloat16), "tensor").astype(jnp.float32),
    )
    reduced = (
        lax.psum_scatter(gain_grads, "dp", scatter_dimension=1, tiled=True),
        lax.psum_scatter(qk_grads, "dp", scatter_dimension=1, tiled=True),
        lax.psum_scatter(query_wgrad, "dp", scatter_dimension=0, tiled=True),
        lax.psum_scatter(keyval_wgrad, "dp", scatter_dimension=0, tiled=True),
        lax.psum_scatter(out_wgrad, "dp", scatter_dimension=1, tiled=True),
        lax.psum_scatter(gate_wgrad, "dp", scatter_dimension=0, tiled=True),
        lax.psum_scatter(up_wgrad, "dp", scatter_dimension=0, tiled=True),
        lax.psum_scatter(down_wgrad, "dp", scatter_dimension=1, tiled=True),
    )
    return (block_out, tokens_grad) + tuple(reduced)


def solution(mesh):
    return jax.shard_map(
        per_device,
        mesh=mesh,
        in_specs=(
            P(("dp", "tensor"), None),
            P("dp"),
            P("dp"),
            P(None, "dp"),
            P(None, "dp"),
            P("dp", "tensor"),
            P("dp", None),
            P("tensor", "dp"),
            P("dp", "tensor"),
            P("dp", "tensor"),
            P("tensor", "dp"),
            P(("dp", "tensor"), None),
        ),
        out_specs=(
            P(("dp", "tensor"), None),
            P(("dp", "tensor"), None),
            P(None, "dp"),
            P(None, "dp"),
            P("dp", "tensor"),
            P("dp", None),
            P("tensor", "dp"),
            P("dp", "tensor"),
            P("dp", "tensor"),
            P("tensor", "dp"),
        ),
        check_vma=False,
    )
```

profile of v0, /device:TPU:0, one launch (start us, length us, event | category | flops | bytes accessed | tf_op | source)
XLA Modules:
  0.0 1072.5 jit_solution(9309093963469955877)
XLA Ops:
  8.0 10.3 all-gather.1
  19.8 8.7 all-gather
  28.6 8.7 all_gather.38
  37.4 9.2 all_gather.41
  47.3 9.4 all_gather.40
  56.7 10.4 all-gather.7.cloned.1.call-done
  67.1 2.5 fusion.48
  69.7 1.9 fusion.123
  74.9 5.0 fusion.103
  82.6 21.6 %while.30 = (s32[]{:T(128)}, bf16[4,512,256]{2,1,0:T(8,128)(2,1)S(1)}, f32[4,512]{1,0:T(4,128)}, s32[4,512]{1,0:T(4,128)S(1)}, s32[4,1024]{1,0:T(4,128)S(1)}, /*...) while((s32[]{:T(128)}, ...), condition=%wide.region_6.7_spmd.clone.clone, body=%wide.region_3.6_spmd.clone.sunk.clone | while | flops 544210432 | bytes 8169585 | solution.py:162
  82.7 1.9 fusion.202
  88.1 1.9 fusion.202
  93.5 1.9 fusion.202
  98.9 1.9 fusion.202
  104.3 3.3 fusion.129
  108.1 92.2 %reduce-scatter.17.cloned.1.call-done = f32[512,640]{1,0:T(8,128)} async-done(((f32[2048,640]{1,0:T(8,128)}), f32[512,640]{1,0:T(8,128)}) %reduce-scatter.17.cloned.1.call-update) | async-done | bytes 1310736 | tf_op jit(solution)/shard_map/reduce_scatter | solution.py:166
  203.7 11.1 %all_gather.43 = bf16[640,512]{1,0:T(8,128)(2,1)} all-gather(bf16[80,512]{1,0:T(8,128)(2,1)S(1)} %copy-done.42), channel_id=1, replica_groups=mesh['dp'=8,'tensor'=4] {'dp'}, dimensions={0}, use_global_device_ids=true | all-gather | bytes 737280 | tf_op jit(solution)/shard_map/all_gather | solution.py:110
  214.8 11.0 %all_gather.44 = bf16[640,512]{1,0:T(8,128)(2,1)} all-gather(bf16[80,512]{1,0:T(8,128)(2,1)S(1)} %copy-done.43), channel_id=1, replica_groups=mesh['dp'=8,'tensor'=4] {'dp'}, dimensions={0}, use_global_device_ids=true | all-gather | bytes 737280 | tf_op jit(solution)/shard_map/all_gather | solution.py:111
  225.8 11.2 %all_gather.45 = bf16[512,640]{0,1:T(8,128)(2,1)} all-gather(bf16[512,80]{0,1:T(8,128)(2,1)} %param.26), channel_id=1, replica_groups=mesh['dp'=8,'tensor'=4] {'dp'}, dimensions={1}, use_global_device_ids=true | all-gather | bytes 737280 | tf_op jit(solution)/shard_map/all_gather | solution.py:112
  237.0 22.1 %all-gather.9.cloned.1.call-done = bf16[2048,640]{1,0:T(8,128)(2,1)} async-done(((bf16[512,640]{1,0:T(8,128)(2,1)}), bf16[2048,640]{1,0:T(8,128)(2,1)}) %all-gather.9.cloned.1.call-update) | async-done | bytes 2621456 | tf_op jit(solution)/shard_map/all_gather | solution.py:171
  259.1 3.8 fusion.130
  263.0 3.9 multiply_convert_fusion.2
  268.3 4.1 fusion.131
  272.5 92.6 %reduce-scatter.19.cloned.1.call-done = f32[512,640]{1,0:T(8,128)} async-done(((f32[2048,640]{1,0:T(8,128)}), f32[512,640]{1,0:T(8,128)}) %reduce-scatter.19.cloned.1.call-update) | async-done | bytes 1310736 | tf_op jit(solution)/shard_map/reduce_scatter | solution.py:176
  365.2 1.6 multiply_reduce_fusion.11
  366.9 1.6 fusion.90
  368.5 1.6 fusion.85
  370.2 55.4 %all-gather.11.cloned.1.call-done = bf16[2048,640]{1,0:T(8,128)(2,1)} async-done(((bf16[512,640]{1,0:T(8,128)(2,1)}), bf16[2048,640]{1,0:T(8,128)(2,1)}) %all-gather.11.cloned.1.call-update) | async-done | bytes 2621456 | tf_op jit(solution)/shard_map/all_gather | solution.py:181
  425.6 8.8 multiply_convert_fusion.1
  434.4 1.8 fusion.132
  436.4 4.1 convolution_add_fusion
  440.6 92.6 %reduce-scatter.21.cloned.1.call-done = f32[512,640]{1,0:T(8,128)} async-done(((f32[2048,640]{1,0:T(8,128)}), f32[512,640]{1,0:T(8,128)}) %reduce-scatter.21.cloned.1.call-update) | async-done | bytes 1310736 | tf_op jit(solution)/shard_map/reduce_scatter | solution.py:186
  533.2 1.9 multiply_reduce_fusion.7
  538.6 55.2 %all-gather.13.cloned.1.call-done = bf16[2048,640]{1,0:T(8,128)(2,1)} async-done(((bf16[512,640]{1,0:T(8,128)(2,1)}), bf16[2048,640]{1,0:T(8,128)(2,1)}) %all-gather.13.cloned.1.call-update) | async-done | bytes 2621456 | tf_op jit(solution)/shard_map/all_gather | solution.py:198
  593.8 3.8 convolution_convert_fusion
  597.6 36.7 %while.31 = (s32[]{:T(128)}, f32[4,512,256]{2,1,0:T(8,128)}, f32[4,1024,256]{2,1,0:T(8,128)}, f32[4,1024,256]{2,1,0:T(8,128)}, s32[4,512]{1,0:T(4,128)S(1)}, /*i...) while((s32[]{:T(128)}, f32[4,512,256]{2,1,0:T(8,128)}, ...), condition=%wide.region_19.20_spmd.clone.clone, body=%wide.region_17.19_spmd.clone.sunk.clone | while | flops 1350565376 | bytes 25201828 | solution.py:216
  601.7 2.5 fusion.216
  610.9 2.4 fusion.216
  620.1 2.4 fusion.216
  629.2 2.4 fusion.216
  635.9 1.9 slice.90
  640.5 4.8 fusion.106
  646.8 1.8 copy-done.1
  652.2 1.8 fusion.82
  654.0 2.6 add_convert_fusion
  658.4 4.1 fusion.83
  662.6 45.1 %reduce-scatter.23.cloned.1.call-done = bf16[512,640]{1,0:T(8,128)(2,1)} async-done(((bf16[2048,640]{1,0:T(8,128)(2,1)}), bf16[512,640]{1,0:T(8,128)(2,1)}) %reduce-scatter.23.cloned.1.call-update) | async-done | bytes 655376 | tf_op jit(solution)/shard_map/reduce_scatter | solution.py:235
  707.7 1.7 fusion.97
  709.5 10.3 all-reduce.9
  721.6 4.5 fusion.136
  726.2 5.2 fusion.134
  731.4 4.4 fusion.135
  735.9 4.2 fusion.133
  740.1 3.9 fusion.121
  744.1 6.3 all-reduce.12.cloned.1.call-done
  750.4 2.3 convert_element_type.112
  754.3 31.8 %reduce-scatter.39.cloned.1.call-done = f32[32,2]{1,0:T(8,128)} async-done(((f32[256,2]{1,0:T(8,128)}), f32[32,2]{1,0:T(8,128)}) %reduce-scatter.39.cloned.1.call-update) | async-done | bytes 272
  787.5 35.8 %reduce-scatter.37.cloned.1.call-done = f32[80,4]{1,0:T(8,128)} async-done(((f32[640,4]{1,0:T(8,128)}), f32[80,4]{1,0:T(8,128)}) %reduce-scatter.37.cloned.1.call-update) | async-done | bytes 1296
  824.7 39.9 %reduce-scatter.35.cloned.1.call-done = f32[512,80]{0,1:T(8,128)} async-done(((f32[512,640]{0,1:T(8,128)}), f32[512,80]{0,1:T(8,128)}) %reduce-scatter.35.cloned.1.call-update) | async-done | bytes 163856 | tf_op jit(solution)/shard_map/reduce_scatter | solution.py:267
  864.6 41.5 %reduce-scatter.31.cloned.1.call-done = f32[80,512]{1,0:T(8,128)} async-done(((f32[640,512]{1,0:T(8,128)}), f32[80,512]{1,0:T(8,128)}) %reduce-scatter.31.cloned.1.call-update) | async-done | bytes 163856 | tf_op jit(solution)/shard_map/reduce_scatter | solution.py:265
  906.1 41.4 %reduce-scatter.33.cloned.1.call-done = f32[80,512]{1,0:T(8,128)} async-done(((f32[640,512]{1,0:T(8,128)}), f32[80,512]{1,0:T(8,128)}) %reduce-scatter.33.cloned.1.call-update) | async-done | bytes 163856 | tf_op jit(solution)/shard_map/reduce_scatter | solution.py:266
  947.5 38.4 %reduce-scatter.29.cloned.1.call-done = f32[256,80]{0,1:T(8,128)} async-done(((f32[256,640]{0,1:T(8,128)}), f32[256,80]{0,1:T(8,128)}) %reduce-scatter.29.cloned.1.call-update) | async-done | bytes 81936 | tf_op jit(solution)/shard_map/reduce_scatter | solution.py:264
  985.9 38.5 %reduce-scatter.25.cloned.1.call-done = f32[80,256]{1,0:T(8,128)} async-done(((f32[640,256]{1,0:T(8,128)}), f32[80,256]{1,0:T(8,128)}) %reduce-scatter.25.cloned.1.call-update) | async-done | bytes 81936 | tf_op jit(solution)/shard_map/reduce_scatter | solution.py:262
  1024.4 41.4 %reduce-scatter.27.cloned.1.call-done = f32[80,512]{1,0:T(8,128)} async-done(((f32[640,512]{1,0:T(8,128)}), f32[80,512]{1,0:T(8,128)}) %reduce-scatter.27.cloned.1.call-update) | async-done | bytes 163856 | tf_op jit(solution)/shard_map/reduce_scatter | solution.py:263
  (272 shorter events, 76.5 us)
Async XLA Ops:
  7.2 40.1 %copy-start.41 = (bf16[80,512]{1,0:T(8,128)(2,1)S(1)}, bf16[80,512]{1,0:T(8,128)(2,1)}, u32[]{:S(2)}) copy-start(bf16[80,512]{1,0:T(8,128)(2,1)} %param.22) | copy-start | bytes 245764
  7.2 59.9 %all-gather.7.cloned.1.call-start = ((), (), s32[]{:S(2)}) async-start(), calls=%async_computation.12 | async-start | bytes 3276800 | tf_op jit(solution)/shard_map/all_gather | solution.py:117
  7.9 192.4 %reduce-scatter.17.cloned.1.call-start = ((), (), s32[]{:S(2)}) async-start(), calls=%async_computation.13 | async-start | bytes 6553600 | tf_op jit(solution)/shard_map/reduce_scatter | solution.py:166
  37.3 34.7 %copy-start.33 = (bf16[640,256]{1,0:T(8,128)(2,1)}, bf16[640,256]{1,0:T(8,128)(2,1)S(1)}, u32[]{:S(2)}) copy-start(bf16[640,256]{1,0:T(8,128)(2,1)S(1)} %all_gather.38) | copy-start | bytes 983044
  46.5 57.7 %copy-start.35 = (bf16[256,640]{0,1:T(8,128)(2,1)}, bf16[256,640]{0,1:T(8,128)(2,1)S(1)}, u32[]{:S(2)}) copy-start(bf16[256,640]{0,1:T(8,128)(2,1)S(1)} %all_gather.41) | copy-start | bytes 983044
  46.5 28.4 %copy-start.50 = (f32[128]{0:T(128)}, f32[128]{0:T(128)S(1)}, u32[]{:S(2)}) copy-start(f32[128]{0:T(128)S(1)} %multiply_power_fusion) | copy-start | bytes 1540
  56.7 14.8 %copy-start.39 = (bf16[640,512]{1,0:T(8,128)(2,1)}, bf16[640,512]{1,0:T(8,128)(2,1)S(1)}, u32[]{:S(2)}) copy-start(bf16[640,512]{1,0:T(8,128)(2,1)S(1)} %all_gather.40) | copy-start | bytes 1966084
  56.7 17.6 %copy-start.46 = (f32[1,256]{1,0:T(1,128)}, f32[1,256]{1,0:T(1,128)S(1)}, u32[]{:S(2)}) copy-start(f32[1,256]{1,0:T(1,128)S(1)} %get-tuple-element.260) | copy-start | bytes 3076
  67.1 2.5 copy-start.27
  69.6 2.4 copy-start.48
  71.5 2.4 copy-start
  104.2 3.3 copy-start.11
  104.2 3.3 copy-start.15
  107.6 94.3 %copy-start.14 = (bf16[512,640]{1,0:T(8,128)(2,1)S(1)}, bf16[512,640]{1,0:T(8,128)(2,1)}, u32[]{:S(2)}) copy-start(bf16[512,640]{1,0:T(8,128)(2,1)} %param.16) | copy-start | bytes 1966084
  107.6 151.5 %all-gather.9.cloned.1.call-start = ((), (), s32[]{:S(2)}) async-start(), calls=%async_computation.14 | async-start | bytes 3276800 | tf_op jit(solution)/shard_map/all_gather | solution.py:171
  200.3 1.7 copy-start.2
  202.5 12.3 %copy-start.43 = (bf16[80,512]{1,0:T(8,128)(2,1)S(1)}, bf16[80,512]{1,0:T(8,128)(2,1)}, u32[]{:S(2)}) copy-start(bf16[80,512]{1,0:T(8,128)(2,1)} %param.25) | copy-start | bytes 245764
  203.6 161.6 %reduce-scatter.19.cloned.1.call-start = ((), (), s32[]{:S(2)}) async-start(), calls=%async_computation.15 | async-start | bytes 6553600 | tf_op jit(solution)/shard_map/reduce_scatter | solution.py:176
  259.1 3.8 copy-start.13
  259.1 3.9 copy-start.25
  262.9 4.0 copy-start.53
  263.0 5.4 copy-start.31
  272.5 153.1 %all-gather.11.cloned.1.call-start = ((), (), s32[]{:S(2)}) async-start(), calls=%async_computation.16 | async-start | bytes 3276800 | tf_op jit(solution)/shard_map/all_gather | solution.py:181
  365.2 1.7 copy-start.10
  365.2 3.4 copy-start.16
  370.2 163.1 %reduce-scatter.21.cloned.1.call-start = ((), (), s32[]{:S(2)}) async-start(), calls=%async_computation.17 | async-start | bytes 6553600 | tf_op jit(solution)/shard_map/reduce_scatter | solution.py:186
  425.6 8.8 copy-start.30
  434.4 1.9 copy-start.7
  434.4 2.0 copy-start.5
  434.4 2.0 copy-start.26
  440.6 153.3 %all-gather.13.cloned.1.call-start = ((), (), s32[]{:S(2)}) async-start(), calls=%async_computation.18 | async-start | bytes 3276800 | tf_op jit(solution)/shard_map/all_gather | solution.py:198
  533.2 1.9 copy-start.17
  533.2 1.9 copy-start.19
  536.0 57.8 %copy-start.36 = (bf16[256,640]{0,1:T(8,128)(2,1)S(1)}, bf16[256,640]{0,1:T(8,128)(2,1)}, u32[]{:S(2)}) copy-start(bf16[256,640]{0,1:T(8,128)(2,1)} %copy-done.35) | copy-start | bytes 983044
  538.4 169.4 %reduce-scatter.23.cloned.1.call-start = ((), (), s32[]{:S(2)}) async-start(), calls=%async_computation.19 | async-start | bytes 3276800 | tf_op jit(solution)/shard_map/reduce_scatter | solution.py:235
  538.6 59.0 %copy-start.12 = (bf16[4,1024,256]{2,1,0:T(8,128)(2,1)S(1)}, bf16[4,1024,256]{2,1,0:T(8,128)(2,1)}, u32[]{:S(2)}) copy-start(bf16[4,1024,256]{2,1,0:T(8,128)(2,1)} %copy-done.11) | copy-start | bytes 6291460
  538.6 59.0 %copy-start.52 = (s32[512]{0:T(512)S(1)}, s32[512]{0:T(512)}, u32[]{:S(2)}) copy-start(s32[512]{0:T(512)} %get-tuple-element.582) | copy-start | bytes 6148
  597.6 2.4 copy-start.18
  606.8 2.4 copy-start.18
  616.0 2.4 copy-start.18
  625.2 2.4 copy-start.18
  635.9 2.8 copy-start.24
  640.5 4.8 copy-start.4
  640.5 4.8 copy-start.47
  646.1 2.6 copy-start.1
  646.8 7.2 copy-start.20
  650.1 2.0 copy-start.40
  652.2 1.8 copy-start.34
  654.0 2.9 copy-start.49
  656.7 1.7 copy-start.28
  656.7 93.7 %all-reduce.12.cloned.1.call-start = ((), (), s32[]{:S(2)}) async-start(), calls=%async_computation.21 | async-start | bytes 1310720 | tf_op jit(solution)/shard_map/psum | solution.py:255
  662.5 59.2 %copy-start.23 = (bf16[2048,512]{1,0:T(8,128)(2,1)S(1)}, bf16[2048,512]{1,0:T(8,128)(2,1)}, u32[]{:S(2)}) copy-start(bf16[2048,512]{1,0:T(8,128)(2,1)} %copy-done.22) | copy-start | bytes 6291460
  662.5 123.6 %reduce-scatter.39.cloned.1.call-start = ((), (), s32[]{:S(2)}) async-start(), calls=%async_computation.28 | async-start | bytes 147456
  720.6 102.7 %reduce-scatter.37.cloned.1.call-start = ((), (), s32[]{:S(2)}) async-start(), calls=%async_computation.27 | async-start | bytes 368640
  721.6 143.0 %reduce-scatter.35.cloned.1.call-start = ((), (), s32[]{:S(2)}) async-start(), calls=%async_computation.26 | async-start | bytes 1474560 | tf_op jit(solution)/shard_map/reduce_scatter | solution.py:267
  726.1 180.0 %reduce-scatter.31.cloned.1.call-start = ((), (), s32[]{:S(2)}) async-start(), calls=%async_computation.24 | async-start | bytes 1474560 | tf_op jit(solution)/shard_map/reduce_scatter | solution.py:265
  726.2 5.2 copy-start.6
  731.4 216.1 %reduce-scatter.33.cloned.1.call-start = ((), (), s32[]{:S(2)}) async-start(), calls=%async_computation.25 | async-start | bytes 1474560 | tf_op jit(solution)/shard_map/reduce_scatter | solution.py:266
  735.8 4.3 copy-start.21
  735.8 250.1 %reduce-scatter.29.cloned.1.call-start = ((), (), s32[]{:S(2)}) async-start(), calls=%async_computation.23 | async-start | bytes 737280 | tf_op jit(solution)/shard_map/reduce_scatter | solution.py:264
  740.1 284.3 %reduce-scatter.25.cloned.1.call-start = ((), (), s32[]{:S(2)}) async-start(), calls=%async_computation.20 | async-start | bytes 737280 | tf_op jit(solution)/shard_map/reduce_scatter | solution.py:262
  744.0 8.8 copy-start.9
  744.0 8.8 copy-start.29
  744.0 321.7 %reduce-scatter.27.cloned.1.call-start = ((), (), s32[]{:S(2)}) async-start(), calls=%async_computation.22 | async-start | bytes 1474560 | tf_op jit(solution)/shard_map/reduce_scatter | solution.py:263
  (10 other events, 11.5 us)
Sparse Core Ops, SparseCore 0:
  9.6 57.4 all-gather.6
  107.7 92.5 reduce-scatter.16
  203.7 55.3 all-gather.8
  272.6 92.5 reduce-scatter.18
  370.3 55.2 all-gather.10
  440.7 92.5 reduce-scatter.20
  538.5 55.3 all-gather.12
  656.8 50.8 reduce-scatter.22
  710.1 40.2 all-reduce.11
  753.2 32.8 reduce-scatter.38
  789.5 33.7 reduce-scatter.36
  827.3 37.2 reduce-scatter.34
  868.8 37.2 reduce-scatter.30
  910.1 37.2 reduce-scatter.32
  951.3 34.5 reduce-scatter.28
  989.7 34.5 reduce-scatter.24
  1028.4 37.3 reduce-scatter.26
where the time goes:
time: 1080 us; the launch traced here: 1070 us
  waiting for transfers between devices  782 us (72%)
  matrix products  113 us (10%)
  blocking collectives  89.9 us (8%)
  other arithmetic  42.5 us (4%)
  local copies, waits for them, and re-layouts  28.3 us (3%)
  between operations  15 us (1%)
    reduce_scatter x1, waiting for transfers between devices, per_device(): lax.psum_scatter(dot_last(gate_grad, w_gate) + dot_last(up_grad, w_up), '...  92.6 us
    reduce_scatter x1, waiting for transfers between devices, per_device(): lax.psum_scatter(dot_plain(hidden, w_down), 'tensor', scatter_dimension=0...  92.6 us
    reduce_scatter x1, waiting for transfers between devices, per_device(): lax.psum_scatter(dot_plain(context, w_out), 'tensor', scatter_dimension=0...  92.2 us
    unnamed x19, waiting for transfers between devices  68.5 us
    all_gather x1, waiting for transfers between devices, per_device(): ffn_grad_rows = lax.all_gather(ffn_grad, 'tensor', axis=0, tiled=True)  55.4 us
    all_gather x1, waiting for transfers between devices, per_device(): lax.all_gather(attn_grad_value.astype(jnp.bfloat16), 'tensor', axis=0, ti...  55.2 us
    reduce_scatter x1, waiting for transfers between devices, per_device(): lax.psum_scatter((dot_last(query_raw_low, w_query) + dot_last(keyval_low,...  45.1 us
    dot_general x18, matrix products, dot_last(): lax.dot_general(left_side, right_side, (((1,), (1,)), ((), ())), preferre...  42.2 us
  transfers between devices with their start and end apart: 17, of which 17 were waited for; matrix products, arithmetic and copies ran while one was open for 4% of the time, Pallas kernels for 0%

commit v1 on v0

v1 whole, which is shorter than its diff:
```python
import jax
import jax.numpy as jnp
from jax import lax
from jax.sharding import PartitionSpec as P

WINDOW = 512
GAIN_COLUMNS = 128


EPSILON = 1e-06
ROPE_BASE = 10000.0
GELU_SCALE = 0.7978845608028654


def norm_rows(values, gain_row):
    return (
        values * lax.rsqrt(jnp.mean(values * values, axis=-1, keepdims=True) + EPSILON) * gain_row
    )


def norm_back(values, gain_row, grad_out):
    inv_rms = lax.rsqrt(jnp.mean(values * values, axis=-1, keepdims=True) + EPSILON)
    weighted = grad_out * gain_row
    inner_mean = jnp.mean(values * weighted, axis=-1, keepdims=True)
    return (
        inv_rms * weighted - values * inv_rms * inv_rms * inv_rms * inner_mean,
        grad_out * values * inv_rms,
    )


def rotate(values, cosine_table, sine_table):
    half_width = values.shape[-1] // 2
    first_half = values[..., :half_width]
    second_half = values[..., half_width:]
    return jnp.concatenate(
        [
            first_half * cosine_table - second_half * sine_table,
            second_half * cosine_table + first_half * sine_table,
        ],
        axis=-1,
    )


def geglu(gate_pre, up_pre):
    inner_term = GELU_SCALE * (gate_pre + 0.044715 * gate_pre * gate_pre * gate_pre)
    return 0.5 * gate_pre * (1.0 + jnp.tanh(inner_term)) * up_pre


def dot_plain(left_side, right_side):
    return jnp.dot(left_side, right_side, preferred_element_type=jnp.float32)


def dot_last(left_side, right_side):
    return lax.dot_general(
        left_side, right_side, (((1,), (1,)), ((), ())), preferred_element_type=jnp.float32
    )


def dot_first(left_side, right_side):
    return lax.dot_general(
        left_side, right_side, (((0,), (0,)), ((), ())), preferred_element_type=jnp.float32
    )


def pack_shards(norm_gains, qk_gains, q_weight, kv_weight, out_weight, gate_weight, up_weight, down_weight):
    rows = q_weight.shape[0]
    kv_columns = kv_weight.shape[1] // lax.axis_size("tensor")
    kv_part = lax.dynamic_slice_in_dim(
        kv_weight, lax.axis_index("tensor") * kv_columns, kv_columns, axis=1
    )
    gain_part = jnp.concatenate(
        [
            norm_gains.T,
            jnp.pad(qk_gains.T, ((0, rows - qk_gains.shape[1]), (0, 0))),
            jnp.zeros((rows, GAIN_COLUMNS - 6), jnp.bfloat16),
        ],
        axis=1,
    )
    return jnp.concatenate(
        [q_weight, out_weight.T, gate_weight, up_weight, down_weight.T, kv_part, gain_part],
        axis=1,
    )


def gather_weights(packed):
    return lax.all_gather(packed, ("tensor", "dp"), axis=0, tiled=True)


def reduce_grads(grads):
    return lax.psum_scatter(
        grads, ("tensor", "dp"), scatter_dimension=0, tiled=True
    ).astype(jnp.float32)


def per_device(
    tokens,
    segments,
    positions,
    norm_gains,
    qk_gains,
    q_weight,
    kv_weight,
    out_weight,
    gate_weight,
    up_weight,
    down_weight,
    cotangent,
):
    parts = lax.axis_size("tensor")
    place = lax.axis_index("tensor")
    rows, width = tokens.shape
    shard_rows = q_weight.shape[0]
    head_width = q_weight.shape[1]
    ff_part = gate_weight.shape[1]
    kv_columns = kv_weight.shape[1]
    kv_part = kv_columns // parts
    qk_rows = qk_gains.shape[1]
    ends = [0]
    for columns in (head_width, head_width, ff_part, ff_part, ff_part, kv_part, GAIN_COLUMNS):
        ends.append(ends[-1] + columns)

    packed = pack_shards(
        norm_gains, qk_gains, q_weight, kv_weight, out_weight, gate_weight, up_weight, down_weight
    )
    gathered = gather_weights(packed).reshape(parts, width, ends[-1])
    halo = lax.ppermute(tokens, "tensor", [(i, i + 1) for i in range(parts - 1)])

    def piece(index):
        return [gathered[t, :, ends[index] : ends[index + 1]] for t in range(parts)]

    w_query, w_out, w_gate, w_up, w_down, w_kv = (piece(i) for i in range(6))
    w_keyval = jnp.concatenate(w_kv, axis=1)
    w_gains = gathered[0, :, ends[6] : ends[7]].astype(jnp.float32)
    gain_table = w_gains[:, :4].T
    qk_table = w_gains.reshape(-1, shard_rows, GAIN_COLUMNS)[:, :qk_rows, 4:6]
    qk_table = qk_table.reshape(head_width, 2).T

    own_input = tokens.astype(jnp.float32)
    both_input = jnp.concatenate([halo, tokens], axis=0).astype(jnp.float32)
    normed_both = norm_rows(both_input, gain_table[0]).astype(jnp.bfloat16)
    normed = normed_both[rows:]
    start = place * rows
    first = jnp.maximum(start - rows, 0)
    own_doc = lax.dynamic_slice_in_dim(segments, start, rows)
    halo_doc = jnp.where(place > 0, lax.dynamic_slice_in_dim(segments, first, rows), -1)
    both_doc = jnp.concatenate([halo_doc, own_doc])
    both_place = jnp.concatenate(
        [
            lax.dynamic_slice_in_dim(positions, first, rows),
            lax.dynamic_slice_in_dim(positions, start, rows),
        ]
    )
    half_width = head_width // 2
    frequency = ROPE_BASE ** (-jnp.arange(half_width, dtype=jnp.float32) * 2.0 / head_width)
    angles = both_place.astype(jnp.float32)[:, None] * frequency[None, :]
    cosine_both = jnp.cos(angles)
    sine_both = jnp.sin(angles)
    cosine_own, sine_own = cosine_both[rows:], sine_both[rows:]

    offsets = jnp.arange(rows)[:, None] + rows - jnp.arange(2 * rows)[None, :]
    allowed = (offsets >= 0) & (offsets < WINDOW) & (own_doc[:, None] == both_doc[None, :])
    score_scale = head_width ** (-0.5)

    keyval_raw = dot_plain(normed_both, w_keyval)
    key_raw = keyval_raw[:, :head_width]
    keys = rotate(norm_rows(key_raw, qk_table[1]), cosine_both, sine_both).astype(jnp.bfloat16)
    value_rows = keyval_raw[:, head_width:].astype(jnp.bfloat16)

    query_raw, queries, lse, context = [], [], [], []
    attn_own = None
    for t in range(parts):
        raw = dot_plain(normed, w_query[t])
        low = rotate(norm_rows(raw, qk_table[0]), cosine_own, sine_own).astype(jnp.bfloat16)
        masked = jnp.where(allowed, dot_last(low, keys) * score_scale, -1000000000.0)
        row_max = jnp.max(masked, axis=1, keepdims=True)
        exponent = jnp.exp(masked - row_max)
        row_total = jnp.sum(exponent, axis=1, keepdims=True)
        probabilities = (exponent / row_total).astype(jnp.bfloat16)
        mixed = dot_plain(probabilities, value_rows).astype(jnp.bfloat16)
        query_raw.append(raw)
        queries.append(low)
        lse.append(row_max + jnp.log(row_total))
        context.append(mixed)
        share = dot_last(mixed, w_out[t])
        attn_own = share if attn_own is None else attn_own + share

    residual = own_input + norm_rows(attn_own, gain_table[1])
    ffn_in = norm_rows(residual, gain_table[2]).astype(jnp.bfloat16)
    gate_pre, up_pre, hidden = [], [], []
    ffn_out = None
    for t in range(parts):
        gate_pre.append(dot_plain(ffn_in, w_gate[t]))
        up_pre.append(dot_plain(ffn_in, w_up[t]))
        hidden.append(geglu(gate_pre[t], up_pre[t]).astype(jnp.bfloat16))
        share = dot_last(hidden[t], w_down[t])
        ffn_out = share if ffn_out is None else ffn_out + share
    block_out = (residual + norm_rows(ffn_out, gain_table[3])).astype(jnp.bfloat16)
    top_grad = cotangent.astype(jnp.float32)
    ffn_grad_value, post_gain_rows = norm_back(ffn_out, gain_table[3], top_grad)
    ffn_grad = ffn_grad_value.astype(jnp.bfloat16)
    ffn_in_grad = None
    grads = [[] for _ in range(parts)]
    down_wgrad, gate_wgrad, up_wgrad = [], [], []
    for t in range(parts):
        hidden_grad = dot_plain(ffn_grad, w_down[t])
        gelu_back = jax.vjp(geglu, gate_pre[t], up_pre[t])[1]
        gate_grad_value, up_grad_value = gelu_back(hidden_grad)
        gate_grad = gate_grad_value.astype(jnp.bfloat16)
        up_grad = up_grad_value.astype(jnp.bfloat16)
        share = dot_last(gate_grad, w_gate[t]) + dot_last(up_grad, w_up[t])
        ffn_in_grad = share if ffn_in_grad is None else ffn_in_grad + share
        gate_wgrad.append(dot_first(ffn_in, gate_grad))
        up_wgrad.append(dot_first(ffn_in, up_grad))
        down_wgrad.append(dot_first(ffn_grad, hidden[t]))
    residual_part, pre_ffn_rows = norm_back(residual, gain_table[2], ffn_in_grad)
    residual_grad = top_grad + residual_part
    attn_grad_value, post_attn_rows = norm_back(attn_own, gain_table[1], residual_grad)
    attn_grad = attn_grad_value.astype(jnp.bfloat16)

    key_grad, value_grad, normed_grad = None, None, None
    query_gain_grad = None
    out_wgrad, query_wgrad = [], []
    for t in range(parts):
        context_grad = dot_plain(attn_grad, w_out[t]).astype(jnp.bfloat16)
        out_wgrad.append(dot_first(attn_grad, context[t]))
        masked = jnp.where(allowed, dot_last(queries[t], keys) * score_scale, -1000000000.0)
        probabilities = jnp.exp(masked - lse[t])
        prob_grad = dot_last(context_grad, value_rows)
        row_delta = jnp.sum(probabilities * prob_grad, axis=1, keepdims=True)
        score_grad = (probabilities * (prob_grad - row_delta) * score_scale).astype(jnp.bfloat16)
        query_grad = dot_plain(score_grad, keys)
        key_share = dot_first(score_grad, queries[t])
        value_share = dot_first(probabilities.astype(jnp.bfloat16), context_grad)
        key_grad = key_share if key_grad is None else key_grad + key_share
        value_grad = value_share if value_grad is None else value_grad + value_share
        unrotated = rotate(query_grad, cosine_own, -sine_own)
        raw_grad, gain_rows = norm_back(query_raw[t], qk_table[0], unrotated)
        gain_share = jnp.sum(gain_rows, axis=0)
        query_gain_grad = gain_share if query_gain_grad is None else query_gain_grad + gain_share
        raw_low = raw_grad.astype(jnp.bfloat16)
        share = dot_last(raw_low, w_query[t])
        normed_grad = share if normed_grad is None else normed_grad + share
        query_wgrad.append(dot_first(normed, raw_low))
    key_raw_grad, key_gain_rows = norm_back(
        key_raw, qk_table[1], rotate(key_grad, cosine_both, -sine_both)
    )
    keyval_low = jnp.concatenate([key_raw_grad, value_grad], axis=1).astype(jnp.bfloat16)
    next_part = lax.ppermute(
        keyval_low[:rows], "tensor", [(i + 1, i) for i in range(parts - 1)]
    )
    keyval_wgrad = dot_first(normed_both, keyval_low)
    keyval_own = (keyval_low[rows:].astype(jnp.float32) + next_part.astype(jnp.float32)).astype(
        jnp.bfloat16
    )
    normed_grad = normed_grad + dot_last(keyval_own, w_keyval)
    input_part, pre_attn_rows = norm_back(own_input, gain_table[0], normed_grad)
    tokens_grad = residual_grad + input_part

    gain_grads = jnp.stack(
        [
            jnp.sum(pre_attn_rows, axis=0),
            jnp.sum(post_attn_rows, axis=0),
            jnp.sum(pre_ffn_rows, axis=0),
            jnp.sum(post_gain_rows, axis=0),
        ],
        axis=1,
    )
    qk_grads = jnp.stack([query_gain_grad, jnp.sum(key_gain_rows, axis=0)], axis=1)
    qk_grads = jnp.pad(
        qk_grads.reshape(-1, qk_rows, 2), ((0, 0), (0, shard_rows - qk_rows), (0, 0))
    ).reshape(width, 2)
    gain_columns = jnp.concatenate(
        [gain_grads, qk_grads, jnp.zeros((width, GAIN_COLUMNS - 6), jnp.float32)], axis=1
    )
    blocks = []
    for t in range(parts):
        blocks.append(
            jnp.concatenate(
                [
                    value.astype(jnp.bfloat16)
                    for value in (
                        query_wgrad[t],
                        out_wgrad[t],
                        gate_wgrad[t],
                        up_wgrad[t],
                        down_wgrad[t],
                        keyval_wgrad[:, t * kv_part : (t + 1) * kv_part],
                        gain_columns if t == 0 else jnp.zeros_like(gain_columns),
                    )
                ],
                axis=1,
            )
        )
    reduced = reduce_grads(jnp.concatenate(blocks, axis=0))
    shared = lax.all_gather(reduced[:, ends[5] :], "tensor", axis=0)
    keyval_out = jnp.concatenate([shared[t, :, :kv_part] for t in range(parts)], axis=1)
    gain_out = shared[0, :, kv_part:]
    cut = [reduced[:, ends[i] : ends[i + 1]] for i in range(5)]
    return (
        block_out,
        tokens_grad,
        gain_out[:, :4].T,
        gain_out[:qk_rows, 4:6].T,
        cut[0],
        keyval_out,
        cut[1].T,
        cut[2],
        cut[3],
        cut[4].T,
    )


def solution(mesh):
    return jax.shard_map(
        per_device,
        mesh=mesh,
        in_specs=(
            P(("dp", "tensor"), None),
            P("dp"),
            P("dp"),
            P(None, "dp"),
            P(None, "dp"),
            P("dp", "tensor"),
            P("dp", None),
            P("tensor", "dp"),
            P("dp", "tensor"),
            P("dp", "tensor"),
            P("tensor", "dp"),
            P(("dp", "tensor"), None),
        ),
        out_specs=(
            P(("dp", "tensor"), None),
            P(("dp", "tensor"), None),
            P(None, "dp"),
            P(None, "dp"),
            P("dp", "tensor"),
            P("dp", None),
            P("tensor", "dp"),
            P("dp", "tensor"),
            P("dp", "tensor"),
            P("tensor", "dp"),
        ),
        check_vma=False,
    )
```

time: 1080 us -> 429 us (0.40)
  waiting for transfers between devices: 782 us -> 237 us
  blocking collectives: 89.9 us -> 14.7 us
  matrix products: 113 us -> 70.6 us
  local copies, waits for them, and re-layouts: 28.3 us -> 46.3 us
    reduce_scatter x10 -> x0, waiting for transfers between devices: 564 us -> none  [the longest x1 92.6 us: per_device(): lax.psum_scatter(dot_last(gate_grad, w_gate) + dot_last(up_grad, w_up), '...]
    unnamed x19 -> x3, waiting for transfers between devices: 68.5 us -> 145 us
    all_gather x4 -> x1, waiting for transfers between devices: 143 us -> 71.1 us  [gather_weights(): return lax.all_gather(packed, ('tensor', 'dp'), axis=0, tiled=True)]
    all_gather x8 -> x1, blocking collectives: 79.6 us -> 14.7 us  [per_device(): shared = lax.all_gather(reduced[:, ends[5]:], 'tensor', axis=0)]
    ppermute x0 -> x2, waiting for transfers between devices: none -> 20.7 us  [the longest x1 20.7 us: per_device(): lax.ppermute(tokens, 'tensor', [(i, i + 1) for i in range(parts - 1)])]
    dot_general x14 -> x29, matrix products: 41.6 us -> 22.3 us  [dot_first(): lax.dot_general(left_side, right_side, (((0,), (0,)), ((), ())), preferre...]
    dot_general x18 -> x29, matrix products: 42.2 us -> 23.6 us  [dot_last(): lax.dot_general(left_side, right_side, (((1,), (1,)), ((), ())), preferre...]
    concatenate x1 -> x5, local copies, waits for them, and re-layouts: 0.01 us -> 13.9 us  [the longest x4 12.1 us: per_device(): jnp.concatenate([value.astype(jnp.bfloat16) for value in (query_wgrad[t],...]
  transfers between devices with their start and end apart: 17 -> 4, of which waited for: 17 -> 3; matrix products, arithmetic and copies ran while one was open for 4% -> 4% of each run, Pallas kernels for 0% -> 0%
where the time goes in v1:
time: 429 us; the launch traced here: 423 us
  waiting for transfers between devices  237 us (55%)
  matrix products  70.6 us (16%)
  local copies, waits for them, and re-layouts  46.3 us (11%)
  other arithmetic  32.3 us (8%)
  between operations  16 us (4%)
  blocking collectives  14.7 us (3%)
  starting transfers between devices  6.59 us (2%)
    unnamed x3, waiting for transfers between devices  145 us
    all_gather x1, waiting for transfers between devices, gather_weights(): return lax.all_gather(packed, ('tensor', 'dp'), axis=0, tiled=True)  71.1 us
    unnamed x131, local copies, waits for them, and re-layouts  28.2 us
    dot_general x29, matrix products, dot_plain(): return jnp.dot(left_side, right_side, preferred_element_type=jnp.float32)  24.7 us
    dot_general x29, matrix products, dot_last(): lax.dot_general(left_side, right_side, (((1,), (1,)), ((), ())), preferre...  23.6 us
    dot_general x29, matrix products, dot_first(): lax.dot_general(left_side, right_side, (((0,), (0,)), ((), ())), preferre...  22.3 us
    ppermute x1, waiting for transfers between devices, per_device(): lax.ppermute(tokens, 'tensor', [(i, i + 1) for i in range(parts - 1)])  20.7 us
    all_gather x1, blocking collectives, per_device(): shared = lax.all_gather(reduced[:, ends[5]:], 'tensor', axis=0)  14.7 us
  transfers between devices with their start and end apart: 4, of which 3 were waited for; matrix products, arithmetic and copies ran while one was open for 4% of the time, Pallas kernels for 0%

profile of v1, /device:TPU:0, one launch (start us, length us, event | category | flops | bytes accessed | tf_op | source)
XLA Modules:
  0.0 423.2 jit_solution(17095274872095438135)
XLA Ops:
  7.2 0.8 copy.57
  8.0 0.8 copy.56
  8.8 1.8 concatenate.83
  10.8 5.0 %collective-permute-start = (bf16[512,640]{1,0:T(8,128)(2,1)}, bf16[512,640]{1,0:T(8,128)(2,1)S(1)}, u32[]{:S(2)}, u32[]{:S(2)}) collective-permute-start(bf16[512,640]{1,0:T(8,128)(2,1)} %param.12), channel_id=1, source_target_pairs={{0,1},{1,2},{2,3},{4,5},{5,6},{6,7},{8,9},{9,10},{10,11},{12,13},{... | collective-permute-start | bytes 1966088 | tf_op jit(solution)/shard_map/ppermute | solution.py:126
  15.8 0.9 dynamic-slice_select_fusion
  16.7 20.7 %collective-permute-done = bf16[512,640]{1,0:T(8,128)(2,1)S(1)} collective-permute-done((bf16[512,640]{1,0:T(8,128)(2,1)}, bf16[512,640]{1,0:T(8,128)(2,1)S(1)}, u32[]{:S(2)}, u32[]{:S(2)}) %collective-permute-start) | collective-permute-done | bytes 655392 | tf_op jit(solution)/shard_map/ppermute | solution.py:126
  37.3 1.4 fusion
  38.8 71.1 %all-gather.3.cloned.1.call-done = bf16[2560,2304]{1,0:T(8,128)(2,1)} async-done(((bf16[80,2304]{1,0:T(8,128)(2,1)}), bf16[2560,2304]{1,0:T(8,128)(2,1)}) %all-gather.3.cloned.1.call-update) | async-done | bytes 11796496 | tf_op jit(solution)/shard_map/all_gather | solution.py:86
  109.8 2.0 fusion.156
  112.9 1.6 multiply_reduce_fusion.24
  114.6 1.4 multiply_reduce_fusion.23
  116.0 1.4 multiply_reduce_fusion.22
  117.4 1.4 multiply_reduce_fusion.25
  119.1 2.3 fusion.129
  121.7 2.3 fusion.116
  124.6 1.0 fusion.164
  126.7 1.0 fusion.162
  129.0 1.0 fusion.165
  131.1 1.0 fusion.163
  133.2 0.9 slice-done.1
  134.1 1.2 slice-done.2
  140.1 0.7 multiply_convert_fusion.12
  140.9 1.0 fusion.100
  141.9 0.7 multiply_convert_fusion.11
  142.6 0.7 multiply_convert_fusion.10
  143.4 0.7 multiply_convert_fusion.9
  147.0 1.4 fusion.34
  148.4 1.5 convolution_convert_fusion.10
  149.9 1.4 multiply_convert_fusion.8
  151.3 1.5 convolution_convert_fusion.12
  153.3 1.4 multiply_convert_fusion.5
  154.8 1.4 multiply_convert_fusion.6
  156.2 1.4 multiply_convert_fusion.7
  157.7 1.5 convolution_convert_fusion.11
  159.1 0.8 convolution_add_fusion.10
  163.1 0.9 multiply_reduce_fusion.4
  164.0 0.9 multiply_reduce_fusion.5
  165.3 1.1 convolution_convert_fusion.20
  175.2 0.8 multiply_convert_fusion.1
  178.9 2.1 fusion.113
  181.7 0.9 fusion.121
  182.9 1.8 convolution_convert_fusion
  185.3 1.3 multiply_reduce_fusion.14
  186.6 1.2 subtract_convert_fusion.2
  187.8 1.1 convolution_convert_fusion.16
  189.6 1.5 collective-permute-start.1
  191.2 1.6 fusion.50
  192.8 1.4 convolution_add_fusion.2
  194.6 1.5 convolution_add_fusion.1
  204.6 2.1 convolution_add_fusion
  207.1 1.8 fusion.46
  209.6 12.0 %concatenate.97 = bf16[640,2304]{0,1:T(8,128)(2,1)S(1)} concatenate(bf16[640,256]{0,1:T(8,128)(2,1)} %convolution_convert_fusion.16, bf16[640,256]{0,1:T(8,128)(2,1)S(1)} %copy-done.20, bf16[640,512]{0,1:T(8,128)(2,1)} %convolution_convert_fusion.12, bf16[640,512]{0,1:T(8,128)(2,1)} %convolution_convert_fusion.11, bf16[640,512]{0,1:T(8,128)(2,1)} %convolution_convert_fusion.10, ...), dimensions={1} | concatenate | bytes 5898240 | tf_op jit(solution)/shard_map/concatenate | solution.py:278
  221.6 8.8 %pad_maximum_fusion = bf16[2560,2304]{0,1:T(8,128)(2,1)} fusion(bf16[640,2304]{0,1:T(8,128)(2,1)} %copy-done.9, bf16[640,2304]{0,1:T(8,128)(2,1)} %copy-done.8, bf16[640,2304]{0,1:T(8,128)(2,1)} %copy-done.7, bf16[640,2304]{0,1:T(8,128)(2,1)S(1)} %concatenate.97), kind=kLoop, calls=%fused_computation | loop fusion | flops 47185920 | bytes 23592960 | tf_op jit(solution)/shard_map/concatenate | solution.py:294
  230.4 15.0 %copy.67 = bf16[2560,2304]{1,0:T(8,128)(2,1)} copy(bf16[2560,2304]{0,1:T(8,128)(2,1)} %pad_maximum_fusion) | data formatting | bytes 23592960
  245.4 1.3 copy-done.3
  247.3 1.5 fusion.43
  248.8 145.0 %reduce-scatter.4.cloned.1.call-done = bf16[80,2304]{1,0:T(8,128)(2,1)} async-done(((bf16[2560,2304]{1,0:T(8,128)(2,1)}), bf16[80,2304]{1,0:T(8,128)(2,1)}) %reduce-scatter.4.cloned.1.call-update) | async-done | bytes 368656
  393.8 1.3 copy.68
  395.2 14.7 %all-gather = f32[320,256]{1,0:T(8,128)S(1)} all-gather(f32[80,256]{1,0:T(8,128)S(1)} %copy.59), channel_id=2, replica_groups=mesh['dp'=8,'tensor'=4] {'tensor'}, dimensions={0}, use_global_device_ids=true | all-gather | bytes 409600 | tf_op jit(solution)/shard_map/all_gather | solution.py:295
  410.1 0.7 copy.62
  412.1 0.8 copy.65
  412.9 0.8 copy.64
  413.7 0.8 copy.66
  414.5 0.7 copy.63
  (261 shorter events, 44.8 us)
Async XLA Ops:
  7.2 1.6 copy-start
  7.2 102.6 %all-gather.3.cloned.1.call-start = ((), (), s32[]{:S(2)}) async-start(), calls=%async_computation.1 | async-start | bytes 12165120 | tf_op jit(solution)/shard_map/all_gather | solution.py:86
  10.7 383.0 %reduce-scatter.4.cloned.1.call-start = ((), (), s32[]{:S(2)}) async-start(), calls=%async_computation.2 | async-start | bytes 12165120
  10.8 26.6 %collective-permute-start = (bf16[512,640]{1,0:T(8,128)(2,1)}, bf16[512,640]{1,0:T(8,128)(2,1)S(1)}, u32[]{:S(2)}, u32[]{:S(2)}) collective-permute-start(bf16[512,640]{1,0:T(8,128)(2,1)} %param.12), channel_id=1, source_target_pairs={{0,1},{1,2},{2,3},{4,5},{5,6},{6,7},{8,9},{9,10},{10,11},{12,13},{... | collective-permute-start | bytes 1966088 | tf_op jit(solution)/shard_map/ppermute | solution.py:126
  38.7 73.8 %copy-start.4 = (bf16[512,640]{1,0:T(8,128)(2,1)S(1)}, bf16[512,640]{1,0:T(8,128)(2,1)}, u32[]{:S(2)}) copy-start(bf16[512,640]{1,0:T(8,128)(2,1)} %param.12) | copy-start | bytes 1966084
  111.8 7.2 %copy-start.50 = (bf16[640,128]{1,0:T(8,128)(2,1)}, bf16[640,128]{1,0:T(8,128)(2,1)S(1)}, u32[]{:S(2)}) copy-start(bf16[640,128]{1,0:T(8,128)(2,1)S(1)} %get-tuple-element.77) | copy-start | bytes 491524
  111.8 7.2 %copy-start.52 = (bf16[640,128]{1,0:T(8,128)(2,1)}, bf16[640,128]{1,0:T(8,128)(2,1)S(1)}, u32[]{:S(2)}) copy-start(bf16[640,128]{1,0:T(8,128)(2,1)S(1)} %get-tuple-element.78) | copy-start | bytes 491524
  111.8 7.2 %copy-start.54 = (bf16[640,128]{1,0:T(8,128)(2,1)}, bf16[640,128]{1,0:T(8,128)(2,1)S(1)}, u32[]{:S(2)}) copy-start(bf16[640,128]{1,0:T(8,128)(2,1)S(1)} %get-tuple-element.79) | copy-start | bytes 491524
  112.9 4.5 %copy-start.16 = (bf16[1024,640]{1,0:T(8,128)(2,1)}, bf16[1024,640]{1,0:T(8,128)(2,1)S(1)}, u32[]{:S(2)}) copy-start(bf16[1024,640]{1,0:T(8,128)(2,1)S(1)} %fusion.2) | copy-start | bytes 3932164
  126.7 9.4 %copy-start.44 = (bf16[512,256]{1,0:T(8,128)(2,1)}, bf16[512,256]{1,0:T(8,128)(2,1)S(1)}, u32[]{:S(2)}) copy-start(bf16[512,256]{1,0:T(8,128)(2,1)S(1)} %convolution_convert_fusion.22) | copy-start | bytes 786436
  130.5 2.7 slice-start
  130.5 3.6 slice-start.1
  131.1 5.4 %copy-start.48 = (bf16[512,256]{1,0:T(8,128)(2,1)}, bf16[512,256]{1,0:T(8,128)(2,1)S(1)}, u32[]{:S(2)}) copy-start(bf16[512,256]{1,0:T(8,128)(2,1)S(1)} %convolution_convert_fusion.21) | copy-start | bytes 786436
  132.6 2.6 slice-start.2
  135.3 0.8 copy-start.46
  142.6 1.5 copy-start.40
  143.4 1.4 copy-start.42
  144.1 1.3 copy-start.26
  145.4 1.1 copy-start.6
  148.4 7.8 %copy-start.23 = (bf16[512,640]{1,0:T(8,128)(2,1)}, bf16[512,640]{1,0:T(8,128)(2,1)S(1)}, u32[]{:S(2)}) copy-start(bf16[512,640]{1,0:T(8,128)(2,1)S(1)} %get-tuple-element.105) | copy-start | bytes 1966084
  154.8 5.2 %copy-start.38 = (bf16[512,512]{1,0:T(8,128)(2,1)}, bf16[512,512]{1,0:T(8,128)(2,1)S(1)}, u32[]{:S(2)}) copy-start(bf16[512,512]{1,0:T(8,128)(2,1)S(1)} %get-tuple-element.82) | copy-start | bytes 1572868
  154.8 8.3 %copy-start.36 = (bf16[512,512]{1,0:T(8,128)(2,1)}, bf16[512,512]{1,0:T(8,128)(2,1)S(1)}, u32[]{:S(2)}) copy-start(bf16[512,512]{1,0:T(8,128)(2,1)S(1)} %get-tuple-element.81) | copy-start | bytes 1572868
  156.2 4.4 %copy-start.34 = (bf16[512,512]{1,0:T(8,128)(2,1)}, bf16[512,512]{1,0:T(8,128)(2,1)S(1)}, u32[]{:S(2)}) copy-start(bf16[512,512]{1,0:T(8,128)(2,1)S(1)} %get-tuple-element.84) | copy-start | bytes 1572868
  156.2 6.2 %copy-start.32 = (bf16[512,512]{1,0:T(8,128)(2,1)}, bf16[512,512]{1,0:T(8,128)(2,1)S(1)}, u32[]{:S(2)}) copy-start(bf16[512,512]{1,0:T(8,128)(2,1)S(1)} %get-tuple-element.83) | copy-start | bytes 1572868
  157.6 3.5 copy-start.30
  157.6 4.2 copy-start.28
  164.8 1.6 copy-start.2
  165.3 2.3 copy-start.10
  174.2 8.4 %copy-start.12 = (bf16[1024,256]{0,1:T(8,128)(2,1)}, bf16[1024,256]{0,1:T(8,128)(2,1)S(1)}, u32[]{:S(2)}) copy-start(bf16[1024,256]{0,1:T(8,128)(2,1)S(1)} %fusion.47) | copy-start | bytes 1572868
  181.4 1.5 copy-start.17
  181.7 3.0 copy-start.14
  189.6 17.1 %collective-permute-start.1 = (bf16[512,512]{0,1:T(8,128)(2,1)}, bf16[512,512]{0,1:T(8,128)(2,1)S(1)}, u32[]{:S(2)}, u32[]{:S(2)}) collective-permute-start(bf16[512,512]{0,1:T(8,128)(2,1)} %fusion.121), channel_id=1, source_target_pairs={{1,0},{2,1},{3,2},{5,4},{6,5},{7,6},{9,8},{10,9},{11,10},{13,12},{... | collective-permute-start | bytes 1572872 | tf_op jit(solution)/shard_map/ppermute | solution.py:248
  191.2 3.0 copy-start.18
  191.2 3.0 copy-start.22
  194.2 1.9 copy-start.21
  194.5 1.9 copy-start.11
  194.6 1.9 copy-start.49
  196.0 1.0 copy-start.39
  196.4 1.3 copy-start.37
  197.1 1.4 copy-start.24
  197.1 1.4 copy-start.27
  197.8 1.4 copy-start.45
  198.5 1.2 copy-start.35
  199.2 1.2 copy-start.33
  199.6 1.4 copy-start.43
  200.3 1.4 copy-start.47
  201.0 1.2 copy-start.31
  201.7 1.2 copy-start.29
  202.2 1.4 copy-start.41
  202.9 1.4 copy-start.25
  204.4 2.4 copy-start.13
  204.4 2.4 copy-start.15
  204.4 2.4 copy-start.51
  204.4 2.3 copy-start.53
  204.4 2.5 copy-start.55
  204.5 2.6 copy-start.56
  204.5 4.4 %copy-start.9 = (bf16[640,2304]{0,1:T(8,128)(2,1)}, bf16[640,2304]{0,1:T(8,128)(2,1)S(1)}, u32[]{:S(2)}) copy-start(bf16[640,2304]{0,1:T(8,128)(2,1)S(1)} %broadcast_dynamic-update-slice_fusion) | copy-start | bytes 8847364
  204.5 4.4 %copy-start.8 = (bf16[640,2304]{0,1:T(8,128)(2,1)}, bf16[640,2304]{0,1:T(8,128)(2,1)S(1)}, u32[]{:S(2)}) copy-start(bf16[640,2304]{0,1:T(8,128)(2,1)S(1)} %broadcast_dynamic-update-slice_fusion.1) | copy-start | bytes 8847364
  204.6 2.2 copy-start.7
  206.7 2.8 copy-start.20
  245.4 1.3 copy-start.3
  245.4 1.5 copy-start.5
  245.4 1.9 copy-start.19
  409.9 6.0 %copy-start.1 = (bf16[80,512]{1,0:T(8,128)(2,1)S(1)}, bf16[80,512]{1,0:T(8,128)(2,1)}, u32[]{:S(2)}) copy-start(bf16[80,512]{1,0:T(8,128)(2,1)} %param.18) | copy-start | bytes 245764
Sparse Core Ops, SparseCore 0:
  11.5 98.2 all-gather.2
  245.5 148.1 reduce-scatter.3

commit v2 on v1

--- a/solution.py
+++ b/solution.py
@@ -1,6 +1,8 @@
 import jax
 import jax.numpy as jnp
 from jax import lax
+from jax.experimental import pallas as pl
+from jax.experimental.pallas import tpu as pltpu
 from jax.sharding import PartitionSpec as P
 
 WINDOW = 512
@@ -90,6 +92,74 @@
     return lax.psum_scatter(
         grads, ("tensor", "dp"), scatter_dimension=0, tiled=True
     ).astype(jnp.float32)
+
+
+def ffn_wgrads(ffn_in, ffn_grad, gate_grad, up_grad, hidden, parts):
+    rows, width = ffn_in.shape
+    columns = gate_grad.shape[1] // parts
+
+    def body(in_ref, grad_ref, gate_ref, up_ref, hidden_ref, out_ref):
+        out_ref[:, :columns] = dot_first(in_ref[...], gate_ref[...]).astype(jnp.bfloat16)
+        out_ref[:, columns : 2 * columns] = dot_first(in_ref[...], up_ref[...]).astype(jnp.bfloat16)
+        out_ref[:, 2 * columns :] = dot_first(grad_ref[...], hidden_ref[...]).astype(jnp.bfloat16)
+
+    whole = pl.BlockSpec((rows, width), lambda t: (0, 0))
+    slab = pl.BlockSpec((rows, columns), lambda t: (0, t))
+    return pl.pallas_call(
+        body,
+        grid=(parts,),
+        in_specs=[whole, whole, slab, slab, slab],
+        out_specs=pl.BlockSpec((width, 3 * columns), lambda t: (t, 0)),
+        out_shape=jax.ShapeDtypeStruct((parts * width, 3 * columns), jnp.bfloat16),
+        compiler_params=pltpu.CompilerParams(vmem_limit_bytes=32 * 1024 * 1024),
+        cost_estimate=pl.CostEstimate(
+            flops=6 * rows * width * columns * parts,
+            bytes_accessed=2 * parts * columns * 3 * (rows + width),
+            transcendentals=0,
+        ),
+        name="ffn_wgrads",
+    )(ffn_in, ffn_grad, gate_grad, up_grad, hidden)
+
+
+def attn_wgrads(normed_both, attn_grad, query_low, context, keyval_low, gain_columns, parts):
+    rows, width = attn_grad.shape
+    columns = query_low.shape[1] // parts
+    kv_part = keyval_low.shape[1] // parts
+
+    def body(normed_ref, grad_ref, query_ref, context_ref, keyval_ref, gain_ref, out_ref):
+        own = normed_ref[rows:, :]
+        out_ref[:, :columns] = dot_first(own, query_ref[...]).astype(jnp.bfloat16)
+        out_ref[:, columns : 2 * columns] = dot_first(grad_ref[...], context_ref[...]).astype(
+            jnp.bfloat16
+        )
+        out_ref[:, 2 * columns : 2 * columns + kv_part] = dot_first(
+            normed_ref[...], keyval_ref[...]
+        ).astype(jnp.bfloat16)
+        out_ref[:, 2 * columns + kv_part :] = gain_ref[...].astype(jnp.bfloat16)
+
+    slab = pl.BlockSpec((rows, columns), lambda t: (0, t))
+    total = 2 * columns + kv_part + gain_columns.shape[1]
+    return pl.pallas_call(
+        body,
+        grid=(parts,),
+        in_specs=[
+            pl.BlockSpec(normed_both.shape, lambda t: (0, 0)),
+            pl.BlockSpec((rows, width), lambda t: (0, 0)),
+            slab,
+            slab,
+            pl.BlockSpec((keyval_low.shape[0], kv_part), lambda t: (0, t)),
+            pl.BlockSpec(gain_columns.shape, lambda t: (0, 0)),
+        ],
+        out_specs=pl.BlockSpec((width, total), lambda t: (t, 0)),
+        out_shape=jax.ShapeDtypeStruct((parts * width, total), jnp.bfloat16),
+        compiler_params=pltpu.CompilerParams(vmem_limit_bytes=32 * 1024 * 1024),
+        cost_estimate=pl.CostEstimate(
+            flops=2 * rows * width * (2 * columns + 2 * kv_part) * parts,
+            bytes_accessed=2 * parts * total * (rows + width),
+            transcendentals=0,
+        ),
+        name="attn_wgrads",
+    )(normed_both, attn_grad, query_low, context, keyval_low, gain_columns)
 
 
 def per_device(
@@ -199,8 +269,7 @@
     ffn_grad_value, post_gain_rows = norm_back(ffn_out, gain_table[3], top_grad)
     ffn_grad = ffn_grad_value.astype(jnp.bfloat16)
     ffn_in_grad = None
-    grads = [[] for _ in range(parts)]
-    down_wgrad, gate_wgrad, up_wgrad = [], [], []
+    gate_grads, up_grads = [], []
     for t in range(parts):
         hidden_grad = dot_plain(ffn_grad, w_down[t])
         gelu_back = jax.vjp(geglu, gate_pre[t], up_pre[t])[1]
@@ -209,20 +278,26 @@
         up_grad = up_grad_value.astype(jnp.bfloat16)
         share = dot_last(gate_grad, w_gate[t]) + dot_last(up_grad, w_up[t])
         ffn_in_grad = share if ffn_in_grad is None else ffn_in_grad + share
-        gate_wgrad.append(dot_first(ffn_in, gate_grad))
-        up_wgrad.append(dot_first(ffn_in, up_grad))
-        down_wgrad.append(dot_first(ffn_grad, hidden[t]))
+        gate_grads.append(gate_grad)
+        up_grads.append(up_grad)
+    ffn_local = ffn_wgrads(
+        ffn_in,
+        ffn_grad,
+        *(jnp.concatenate(group, axis=1) for group in (gate_grads, up_grads, hidden)),
+        parts,
+    )
     residual_part, pre_ffn_rows = norm_back(residual, gain_table[2], ffn_in_grad)
     residual_grad = top_grad + residual_part
     attn_grad_value, post_attn_rows = norm_back(attn_own, gain_table[1], residual_grad)
     attn_grad = attn_grad_value.astype(jnp.bfloat16)
+    attn_grad, ffn_local = lax.optimization_barrier((attn_grad, ffn_local))
+    ffn_reduced = reduce_grads(ffn_local)
 
     key_grad, value_grad, normed_grad = None, None, None
     query_gain_grad = None
-    out_wgrad, query_wgrad = [], []
+    raw_lows = []
     for t in range(parts):
         context_grad = dot_plain(attn_grad, w_out[t]).astype(jnp.bfloat16)
-        out_wgrad.append(dot_first(attn_grad, context[t]))
         masked = jnp.where(allowed, dot_last(queries[t], keys) * score_scale, -1000000000.0)
         probabilities = jnp.exp(masked - lse[t])
         prob_grad = dot_last(context_grad, value_rows)
@@ -240,7 +315,7 @@
         raw_low = raw_grad.astype(jnp.bfloat16)
         share = dot_last(raw_low, w_query[t])
         normed_grad = share if normed_grad is None else normed_grad + share
-        query_wgrad.append(dot_first(normed, raw_low))
+        raw_lows.append(raw_low)
     key_raw_grad, key_gain_rows = norm_back(
         key_raw, qk_table[1], rotate(key_grad, cosine_both, -sine_both)
     )
@@ -248,7 +323,6 @@
     next_part = lax.ppermute(
         keyval_low[:rows], "tensor", [(i + 1, i) for i in range(parts - 1)]
     )
-    keyval_wgrad = dot_first(normed_both, keyval_low)
     keyval_own = (keyval_low[rows:].astype(jnp.float32) + next_part.astype(jnp.float32)).astype(
         jnp.bfloat16
     )
@@ -272,41 +346,31 @@
     gain_columns = jnp.concatenate(
         [gain_grads, qk_grads, jnp.zeros((width, GAIN_COLUMNS - 6), jnp.float32)], axis=1
     )
-    blocks = []
-    for t in range(parts):
-        blocks.append(
-            jnp.concatenate(
-                [
-                    value.astype(jnp.bfloat16)
-                    for value in (
-                        query_wgrad[t],
-                        out_wgrad[t],
-                        gate_wgrad[t],
-                        up_wgrad[t],
-                        down_wgrad[t],
-                        keyval_wgrad[:, t * kv_part : (t + 1) * kv_part],
-                        gain_columns if t == 0 else jnp.zeros_like(gain_columns),
-                    )
-                ],
-                axis=1,
-            )
-        )
-    reduced = reduce_grads(jnp.concatenate(blocks, axis=0))
-    shared = lax.all_gather(reduced[:, ends[5] :], "tensor", axis=0)
+    attn_local = attn_wgrads(
+        normed_both,
+        attn_grad,
+        jnp.concatenate(raw_lows, axis=1),
+        jnp.concatenate(context, axis=1),
+        keyval_low,
+        gain_columns,
+        parts,
+    )
+    attn_local, ffn_reduced = lax.optimization_barrier((attn_local, ffn_reduced))
+    attn_reduced = reduce_grads(attn_local)
+    shared = lax.all_gather(attn_reduced[:, 2 * head_width :], "tensor", axis=0)
     keyval_out = jnp.concatenate([shared[t, :, :kv_part] for t in range(parts)], axis=1)
     gain_out = shared[0, :, kv_part:]
-    cut = [reduced[:, ends[i] : ends[i + 1]] for i in range(5)]
     return (
         block_out,
         tokens_grad,
         gain_out[:, :4].T,
         gain_out[:qk_rows, 4:6].T,
-        cut[0],
+        attn_reduced[:, :head_width],
         keyval_out,
-        cut[1].T,
-        cut[2],
-        cut[3],
-        cut[4].T,
+        attn_reduced[:, head_width : 2 * head_width].T,
+        ffn_reduced[:, :ff_part],
+        ffn_reduced[:, ff_part : 2 * ff_part],
+        ffn_reduced[:, 2 * ff_part :].T,
     )
 
 

time: 429 us -> 470 us (1.096)
  waiting for transfers between devices: 237 us -> 254 us
  local copies, waits for them, and re-layouts: 46.3 us -> 58.5 us
  Pallas kernels: 0 us -> 9.43 us
    reduce_scatter x0 -> x2, waiting for transfers between devices: none -> 164 us  [reduce_grads(): lax.psum_scatter(grads, ('tensor', 'dp'), scatter_dimension=0, tiled=True)]
    unnamed x3, waiting for transfers between devices: 145 us -> 0.05 us
    dot_general x29 -> x8, matrix products: 22.3 us -> 5.52 us  [dot_first(): lax.dot_general(left_side, right_side, (((0,), (0,)), ((), ())), preferre...]
    dot_general x29, matrix products: 24.7 us -> 36 us  [dot_plain(): return jnp.dot(left_side, right_side, preferred_element_type=jnp.float32)]
    pallas_call x0 -> x2, Pallas kernels: none -> 9.43 us  [the longest x1 5.4 us: ffn_wgrads(): pl.pallas_call(body, grid=(parts,), in_specs=[whole, whole, slab, slab, s...]
    concatenate x4 -> x1, local copies, waits for them, and re-layouts: 12.1 us -> 2.73 us  [per_device(): jnp.concatenate([gain_grads, qk_grads, jnp.zeros((width, GAIN_COLUMNS - 6...]
    dot_general x0 -> x4, local copies, waits for them, and re-layouts: none -> 7.57 us  [dot_plain(): return jnp.dot(left_side, right_side, preferred_element_type=jnp.float32)]
    concatenate x1 -> x5, other arithmetic: 8.82 us -> 2.14 us  [the longest x1 1.12 us: per_device(): jnp.concatenate(raw_lows, axis=1)]
  transfers between devices with their start and end apart: 4 -> 5, of which waited for: 3 -> 4; matrix products, arithmetic and copies ran while one was open for 4% -> 10% of each run, Pallas kernels for 0% -> 1%
where the time goes in v2:
time: 470 us; the launch traced here: 463 us
  waiting for transfers between devices  254 us (54%)
  matrix products  67.6 us (14%)
  local copies, waits for them, and re-layouts  58.5 us (12%)
  other arithmetic  35.5 us (8%)
  between operations  16.6 us (4%)
  blocking collectives  14.6 us (3%)
  Pallas kernels  9.43 us (2%)
  starting transfers between devices  6.5 us (1%)
    reduce_scatter x2, waiting for transfers between devices, reduce_grads(): lax.psum_scatter(grads, ('tensor', 'dp'), scatter_dimension=0, tiled=True)  164 us
    all_gather x1, waiting for transfers between devices, gather_weights(): return lax.all_gather(packed, ('tensor', 'dp'), axis=0, tiled=True)  71.1 us
    dot_general x29, matrix products, dot_plain(): return jnp.dot(left_side, right_side, preferred_element_type=jnp.float32)  36 us
    unnamed x296, local copies, waits for them, and re-layouts  33.9 us
    dot_general x29, matrix products, dot_last(): lax.dot_general(left_side, right_side, (((1,), (1,)), ((), ())), preferre...  26.1 us
    ppermute x1, waiting for transfers between devices, per_device(): lax.ppermute(tokens, 'tensor', [(i, i + 1) for i in range(parts - 1)])  19 us
    all_gather x1, blocking collectives, per_device(): shared = lax.all_gather(attn_reduced[:, 2 * head_width:], 'tensor', axis=0)  14.6 us
  transfers between devices with their start and end apart: 5, of which 4 were waited for; matrix products, arithmetic and copies ran while one was open for 10% of the time, Pallas kernels for 1%

profile of v2, /device:TPU:0, one launch (start us, length us, event | category | flops | bytes accessed | tf_op | source)
XLA Modules:
  0.0 462.8 jit_solution(15388871224988073962)
XLA Ops:
  8.8 1.8 concatenate.82
  10.7 5.0 %collective-permute-start = (bf16[512,640]{1,0:T(8,128)(2,1)}, bf16[512,640]{1,0:T(8,128)(2,1)S(1)}, u32[]{:S(2)}, u32[]{:S(2)}) collective-permute-start(bf16[512,640]{1,0:T(8,128)(2,1)} %param.12), channel_id=1, source_target_pairs={{0,1},{1,2},{2,3},{4,5},{5,6},{6,7},{8,9},{9,10},{10,11},{12,13},{... | collective-permute-start | bytes 1966088 | tf_op jit(solution)/shard_map/ppermute | solution.py:196
  18.3 19.0 %collective-permute-done = bf16[512,640]{1,0:T(8,128)(2,1)S(1)} collective-permute-done((bf16[512,640]{1,0:T(8,128)(2,1)}, bf16[512,640]{1,0:T(8,128)(2,1)S(1)}, u32[]{:S(2)}, u32[]{:S(2)}) %collective-permute-start) | collective-permute-done | bytes 655392 | tf_op jit(solution)/shard_map/ppermute | solution.py:196
  37.3 1.4 fusion
  38.7 71.1 %all-gather.3.cloned.1.call-done = bf16[2560,2304]{1,0:T(8,128)(2,1)} async-done(((bf16[80,2304]{1,0:T(8,128)(2,1)}), bf16[2560,2304]{1,0:T(8,128)(2,1)}) %all-gather.3.cloned.1.call-update) | async-done | bytes 11796496 | tf_op jit(solution)/shard_map/all_gather | solution.py:88
  109.8 1.3 fusion.133
  111.2 1.0 slice_reduce_fusion
  112.7 2.8 multiply_reduce_fusion.22
  115.4 2.8 multiply_reduce_fusion.23
  118.2 2.7 multiply_reduce_fusion.24
  120.9 2.7 multiply_reduce_fusion.25
  124.7 1.3 copy-done.19
  126.1 1.0 slice.322
  127.1 1.6 copy.305
  129.8 1.2 copy.200
  131.1 2.3 copy.196
  133.3 2.0 copy.198
  135.4 2.0 copy.192
  138.6 2.8 fusion.101
  142.1 1.2 copy-done.126
  144.9 2.0 copy-done.20
  147.5 1.4 slice-done.2
  157.9 1.1 multiply_reduce_fusion.9
  168.1 1.1 fusion.28
  169.2 1.4 fusion.25
  170.6 1.4 multiply_convert_fusion.8
  172.6 1.4 multiply_convert_fusion.7
  174.6 1.4 multiply_convert_fusion.6
  176.6 1.4 multiply_convert_fusion.5
  181.6 1.5 multiply_reduce_fusion.4
  183.1 1.4 multiply_reduce_fusion.5
  185.5 5.4 %ffn_wgrads.1 = bf16[2560,1536]{1,0:T(8,128)(2,1)S(1)} custom-call(bf16[512,640]{1,0:T(8,128)(2,1)S(1)} %multiply_convert_fusion.4.in_ref, bf16[512,640]{1,0:T(8,128)(2,1)S(1)} %get-tuple-element.103.grad_ref, bf16[512,2048]{1,0:T(8,128)(2,1)S(1)} %pad_maximum_fusion.gate_ref, bf16[512,2048]{1,0:T(8,128)(2,1)S(1)} %pad_maximum_fusion.1.up_ref, ...), custom_call_target="tpu_custom_call" | custom-call | flops 4026531840 | bytes 14155776 | tf_op jit(solution)/shard_map/ffn_wgrads/pallas_call | solution.py:108
  190.9 3.0 copy-done.2
  194.0 2.2 convolution_convert_fusion.4
  196.2 1.5 convolution_convert_fusion.7
  197.7 2.1 convolution_convert_fusion.5
  199.8 2.1 convolution_convert_fusion.6
  204.1 1.5 fusion.117
  205.6 1.5 copy-done.12
  207.1 1.9 multiply_reduce_fusion.2
  211.4 1.2 copy-done.14
  215.2 1.2 copy-done.16
  218.6 2.5 fusion.98
  227.0 1.4 collective-permute-start.1
  231.2 1.6 fusion.130
  236.7 1.7 multiply_reduce_fusion.14
  239.7 1.5 pad_maximum_fusion.3.keyval_ref
  242.5 1.1 pad_maximum_fusion.6.query_ref
  243.6 1.4 fusion.115
  245.0 1.4 convolution_add_fusion.2
  246.4 1.4 convolution_add_fusion.1
  247.9 1.5 convolution_add_fusion
  249.5 2.9 fusion.37
  254.1 2.7 concatenate.101.gain_ref
  256.8 1.2 copy-done.4
  258.0 1.1 copy-done.6
  260.1 4.0 attn_wgrads.1
  264.1 1.9 copy-done.3
  266.0 60.5 %reduce-scatter.3.cloned.1.call-done = bf16[80,1536]{1,0:T(8,128)(2,1)} async-done(((bf16[2560,1536]{1,0:T(8,128)(2,1)}), bf16[80,1536]{1,0:T(8,128)(2,1)}) %reduce-scatter.3.cloned.1.call-update) | async-done | bytes 245776 | tf_op jit(solution)/shard_map/reduce_scatter | solution.py:92
  327.5 1.3 copy-done.24
  329.0 2.8 fusion.34
  332.6 103.5 %reduce-scatter.5.cloned.1.call-done = bf16[80,768]{1,0:T(8,128)(2,1)} async-done(((bf16[2560,768]{1,0:T(8,128)(2,1)}), bf16[80,768]{1,0:T(8,128)(2,1)}) %reduce-scatter.5.cloned.1.call-update) | async-done | bytes 122896 | tf_op jit(solution)/shard_map/reduce_scatter | solution.py:92
  436.1 1.4 fusion.134
  437.5 14.6 %all-gather = f32[320,256]{1,0:T(8,128)S(1)} all-gather(f32[80,256]{1,0:T(8,128)S(1)} %get-tuple-element.127), channel_id=2, replica_groups=mesh['dp'=8,'tensor'=4] {'tensor'}, dimensions={0}, use_global_device_ids=true | all-gather | bytes 409600 | tf_op jit(solution)/shard_map/all_gather | solution.py:360
  (415 shorter events, 66.5 us)
Async XLA Ops:
  7.2 102.6 %all-gather.3.cloned.1.call-start = ((), (), s32[]{:S(2)}) async-start(), calls=%async_computation.2 | async-start | bytes 12165120 | tf_op jit(solution)/shard_map/all_gather | solution.py:88
  10.7 315.8 %reduce-scatter.3.cloned.1.call-start = ((), (), s32[]{:S(2)}) async-start(), calls=%async_computation.3 | async-start | bytes 8110080 | tf_op jit(solution)/shard_map/reduce_scatter | solution.py:92
  10.7 26.5 %collective-permute-start = (bf16[512,640]{1,0:T(8,128)(2,1)}, bf16[512,640]{1,0:T(8,128)(2,1)S(1)}, u32[]{:S(2)}, u32[]{:S(2)}) collective-permute-start(bf16[512,640]{1,0:T(8,128)(2,1)} %param.12), channel_id=1, source_target_pairs={{0,1},{1,2},{2,3},{4,5},{5,6},{6,7},{8,9},{9,10},{10,11},{12,13},{... | collective-permute-start | bytes 1966088 | tf_op jit(solution)/shard_map/ppermute | solution.py:196
  17.6 93.5 %copy-start.125 = (s32[512]{0:T(512)}, s32[512]{0:T(512)S(1)}, u32[]{:S(2)}) copy-start(s32[512]{0:T(512)S(1)} %get-tuple-element.129) | copy-start | bytes 6148
  38.7 73.6 %copy-start.25 = (bf16[512,640]{1,0:T(8,128)(2,1)S(1)}, bf16[512,640]{1,0:T(8,128)(2,1)}, u32[]{:S(2)}) copy-start(bf16[512,640]{1,0:T(8,128)(2,1)} %param.12) | copy-start | bytes 1966084
  111.2 12.5 %copy-start.97 = (bf16[640,128]{1,0:T(8,128)(2,1)}, bf16[640,128]{1,0:T(8,128)(2,1)S(1)}, u32[]{:S(2)}) copy-start(bf16[640,128]{1,0:T(8,128)(2,1)S(1)} %get-tuple-element.75) | copy-start | bytes 491524
  111.2 12.5 %copy-start.99 = (bf16[640,128]{1,0:T(8,128)(2,1)}, bf16[640,128]{1,0:T(8,128)(2,1)S(1)}, u32[]{:S(2)}) copy-start(bf16[640,128]{1,0:T(8,128)(2,1)S(1)} %get-tuple-element.76) | copy-start | bytes 491524
  111.2 12.5 %copy-start.101 = (bf16[640,128]{1,0:T(8,128)(2,1)}, bf16[640,128]{1,0:T(8,128)(2,1)S(1)}, u32[]{:S(2)}) copy-start(bf16[640,128]{1,0:T(8,128)(2,1)S(1)} %get-tuple-element.77) | copy-start | bytes 491524
  111.2 12.5 %copy-start.103 = (bf16[640,128]{1,0:T(8,128)(2,1)}, bf16[640,128]{1,0:T(8,128)(2,1)S(1)}, u32[]{:S(2)}) copy-start(bf16[640,128]{1,0:T(8,128)(2,1)S(1)} %get-tuple-element.78) | copy-start | bytes 491524
  112.3 3.1 copy-start.105
  128.7 8.8 %copy-start.17 = (f32[1024,256]{1,0:T(8,128)}, f32[1024,256]{1,0:T(8,128)S(1)}, u32[]{:S(2)}) copy-start(f32[1024,256]{1,0:T(8,128)S(1)} %copy.305) | copy-start | bytes 3145732
  131.1 10.4 %copy-start.28 = (f32[512,256]{1,0:T(8,128)}, f32[512,256]{1,0:T(8,128)S(1)}, u32[]{:S(2)}) copy-start(f32[512,256]{1,0:T(8,128)S(1)} %copy.200) | copy-start | bytes 1572868
  137.4 4.1 copy-start.31
  137.5 4.1 copy-start.34
  137.5 4.1 copy-start.37
  137.5 4.1 copy-start.119
  138.5 3.4 copy-start.108
  138.5 3.4 copy-start.115
  138.6 3.3 copy-start.110
  138.6 3.3 copy-start.112
  141.4 7.8 %copy-start.44 = (f32[1024,128]{1,0:T(8,128)}, f32[1024,128]{1,0:T(8,128)S(1)}, u32[]{:S(2)}) copy-start(f32[1024,128]{1,0:T(8,128)S(1)} %get-tuple-element.132) | copy-start | bytes 1572868
  141.5 7.8 %copy-start.46 = (f32[1024,128]{1,0:T(8,128)}, f32[1024,128]{1,0:T(8,128)S(1)}, u32[]{:S(2)}) copy-start(f32[1024,128]{1,0:T(8,128)S(1)} %get-tuple-element.133) | copy-start | bytes 1572868
  141.5 12.7 %copy-start.93 = (bf16[1024,128]{1,0:T(8,128)(2,1)}, bf16[1024,128]{1,0:T(8,128)(2,1)S(1)}, u32[]{:S(2)}) copy-start(bf16[1024,128]{1,0:T(8,128)(2,1)S(1)} %get-tuple-element.107) | copy-start | bytes 786436
  141.5 12.7 %copy-start.95 = (bf16[1024,128]{1,0:T(8,128)(2,1)}, bf16[1024,128]{1,0:T(8,128)(2,1)S(1)}, u32[]{:S(2)}) copy-start(bf16[1024,128]{1,0:T(8,128)(2,1)S(1)} %get-tuple-element.108) | copy-start | bytes 786436
  141.5 5.9 %slice-start = ((s8[11796480]{0:T(1024)(128)(4,1)}), s8[4194304]{0:T(1024)(128)(4,1)S(1)}, s32[]{:S(2)}) async-start(s8[11796480]{0:T(1024)(128)(4,1)} %bitcast.220), calls=%async_computation.5 | async-start | bytes 8388608
  142.1 9.8 %copy-start.83 = (bf16[512,128]{1,0:T(8,128)(2,1)}, bf16[512,128]{1,0:T(8,128)(2,1)S(1)}, u32[]{:S(2)}) copy-start(bf16[512,128]{1,0:T(8,128)(2,1)S(1)} %get-tuple-element.98) | copy-start | bytes 393220
  143.4 4.1 slice-start.1
  144.3 3.1 copy-start.8
  144.3 2.6 copy-start.20
  149.5 4.7 %copy-start.85 = (bf16[512,128]{1,0:T(8,128)(2,1)}, bf16[512,128]{1,0:T(8,128)(2,1)S(1)}, u32[]{:S(2)}) copy-start(bf16[512,128]{1,0:T(8,128)(2,1)S(1)} %get-tuple-element.95) | copy-start | bytes 393220
  149.5 4.7 %copy-start.87 = (bf16[512,128]{1,0:T(8,128)(2,1)}, bf16[512,128]{1,0:T(8,128)(2,1)S(1)}, u32[]{:S(2)}) copy-start(bf16[512,128]{1,0:T(8,128)(2,1)S(1)} %get-tuple-element.96) | copy-start | bytes 393220
  151.9 4.4 copy-start.75
  154.1 2.8 copy-start.77
  179.2 23.3 %copy-start.117 = (f32[512]{0:T(512)}, f32[512]{0:T(512)S(1)}, u32[]{:S(2)}) copy-start(f32[512]{0:T(512)S(1)} %log_add_fusion.3) | copy-start | bytes 6148
  185.5 14.3 %copy-start.5 = (bf16[512,640]{1,0:T(8,128)(2,1)}, bf16[512,640]{1,0:T(8,128)(2,1)S(1)}, u32[]{:S(2)}) copy-start(bf16[512,640]{1,0:T(8,128)(2,1)S(1)} %subtract_convert_fusion.grad_ref) | copy-start | bytes 1966084
  190.9 3.0 copy-start.2
  194.0 5.9 %copy-start.132 = (f32[512]{0:T(512)S(1)}, f32[512]{0:T(512)}, u32[]{:S(2)}) copy-start(f32[512]{0:T(512)} %copy-done.131) | copy-start | bytes 6148
  194.0 7.9 %copy-start.21 = (f32[1024,512]{0,1:T(8,128)S(1)}, f32[1024,512]{0,1:T(8,128)}, u32[]{:S(2)}) copy-start(f32[1024,512]{0,1:T(8,128)} %copy-done.19) | copy-start | bytes 6291460
  196.2 5.7 %copy-start.9 = (f32[512,1024]{1,0:T(8,128)S(1)}, f32[512,1024]{1,0:T(8,128)}, u32[]{:S(2)}) copy-start(f32[512,1024]{1,0:T(8,128)} %copy-done.8) | copy-start | bytes 6291460
  197.7 4.8 %copy-start.72 = (bf16[512,256]{1,0:T(8,128)(2,1)}, bf16[512,256]{1,0:T(8,128)(2,1)S(1)}, u32[]{:S(2)}) copy-start(bf16[512,256]{1,0:T(8,128)(2,1)S(1)} %convolution_convert_fusion.7) | copy-start | bytes 786436
  205.6 230.5 %reduce-scatter.5.cloned.1.call-start = ((), (), s32[]{:S(2)}) async-start(), calls=%async_computation.4 | async-start | bytes 4055040 | tf_op jit(solution)/shard_map/reduce_scatter | solution.py:92
  209.0 2.3 copy-start.22
  210.3 2.3 copy-start.14
  218.0 3.1 copy-start.53
  218.0 3.1 copy-start.18
  218.0 3.1 copy-start.121
  222.8 3.2 copy-start.40
  225.3 3.2 copy-start.123
  225.3 4.0 copy-start.124
  226.0 4.1 copy-start.122
  226.1 5.1 %copy-start.56 = (bf16[512,1024]{1,0:T(8,128)(2,1)S(1)}, bf16[512,1024]{1,0:T(8,128)(2,1)}, u32[]{:S(2)}) copy-start(bf16[512,1024]{1,0:T(8,128)(2,1)} %copy-done.55) | copy-start | bytes 3145732
  226.1 6.7 %copy-start.52 = (bf16[512,1024]{1,0:T(8,128)(2,1)S(1)}, bf16[512,1024]{1,0:T(8,128)(2,1)}, u32[]{:S(2)}) copy-start(bf16[512,1024]{1,0:T(8,128)(2,1)} %copy-done.51) | copy-start | bytes 3145732
  227.0 22.4 %collective-permute-start.1 = (bf16[512,512]{1,0:T(8,128)(2,1)}, bf16[512,512]{1,0:T(8,128)(2,1)}, u32[]{:S(2)}, u32[]{:S(2)}) collective-permute-start(bf16[512,512]{1,0:T(8,128)(2,1)} %fusion.106), channel_id=1, source_target_pairs={{1,0},{2,1},{3,2},{5,4},{6,5},{7,6},{9,8},{10,9},{11,10},{13,12},{... | collective-permute-start | bytes 1572872 | tf_op jit(solution)/shard_map/ppermute | solution.py:323
  233.5 2.5 copy-start.57
  233.5 2.5 copy-start.59
  235.9 2.5 copy-start.61
  235.9 2.5 copy-start.63
  235.9 2.5 copy-start.65
  236.0 2.5 copy-start.67
  236.7 2.7 copy-start.76
  236.7 2.7 copy-start.78
  236.7 2.7 copy-start.80
  236.7 2.7 copy-start.82
  329.0 126.9 %copy-start.1 = (bf16[80,512]{1,0:T(8,128)(2,1)S(1)}, bf16[80,512]{1,0:T(8,128)(2,1)}, u32[]{:S(2)}) copy-start(bf16[80,512]{1,0:T(8,128)(2,1)} %param.18) | copy-start | bytes 245764
  (86 other events, 122.2 us)
Sparse Core Ops, SparseCore 0:
  11.5 98.2 all-gather.2
  205.7 120.7 reduce-scatter.2
  332.8 103.2 reduce-scatter.4
